TPU v7x, 32 devices: a whole 2x2x4 slice. The times are simulated.
32 devices in a mesh: ctx: 8 (over z, x), wsh: 4 (over y, core).
Axes of the slice: x: 2, y: 2, z: 4, core: 2. Of those that a mesh axis runs over, the one named last changes fastest.
Arguments:
- inputs: bfloat16 [8, 1024, 768], P('wsh', 'ctx'), may hold values from -6 to 6
- teacher: bfloat16 [8, 1024, 768], P('wsh', 'ctx'), may hold values from -6 to 6
- seq_lengths: int32 [8], P('wsh'), may hold values from 256 to 1024, as said below
- gain_attn: bfloat16 [768], P('wsh'), may hold values from 0.5 to 1.5
- w_query: bfloat16 [768, 768], P('wsh'), may hold values from -0.109375 to 0.109375
- w_key: bfloat16 [768, 768], P('wsh'), may hold values from -0.109375 to 0.109375
- w_value: bfloat16 [768, 768], P('wsh'), may hold values from -0.21875 to 0.21875
- w_out: bfloat16 [768, 768], P('wsh'), may hold values from -2.5 to 2.5
- bias_table: bfloat16 [32, 12], P('wsh'), may hold values from -4 to 4
- gain_ffn: bfloat16 [768], P('wsh'), may hold values from 0.5 to 1.5
- w_inner: bfloat16 [768, 3072], P('wsh'), may hold values from -0.21875 to 0.21875
- w_outer: bfloat16 [3072, 768], P('wsh'), may hold values from -0.109375 to 0.109375
Outputs:
- layer_out: bfloat16 [8, 1024, 768], P('wsh', 'ctx')
- loss_value: float32 [], replicated
- input_grad: float32 [8, 1024, 768], P('wsh', 'ctx')
- gain_attn_grad: float32 [768], P('wsh')
- w_query_grad: float32 [768, 768], P('wsh')
- w_key_grad: float32 [768, 768], P('wsh')
- w_value_grad: float32 [768, 768], P('wsh')
- w_out_grad: float32 [768, 768], P('wsh')
- bias_table_grad: float32 [32, 12], P('wsh')
- gain_ffn_grad: float32 [768], P('wsh')
- w_inner_grad: float32 [768, 3072], P('wsh')
- w_outer_grad: float32 [3072, 768], P('wsh')
Inputs may be any that keep to these rules, and one draw needn't show every extreme that they name: `seq_lengths`: in each aligned group of 2 sequences exactly one, chosen by the seed, has all 1024 tokens valid; every other sequence has fewer.
All inputs are finite; a program needn't handle non-finite values.
Results may differ from a plain program's by a relative error of at most 0.017.
Values may be sent and summed in bfloat16 or wider, within the bound.
No kernel may reach another device: no remote copies, remote signals or barrier semaphores. Data moves between devices by JAX's collectives and lax.ppermute only.
A program may use at most 128 MiB of HBM per device.

v0:
```python
import jax
import jax.numpy as jnp
from jax import lax
from jax.sharding import PartitionSpec as P

D = 768
H = 12
DH = 64
BUCKETS = 32
SEQ_DEV = 2
PIECE = 128


EPS = 1e-06
NEG_FILL = -1e30
BUCKET_EDGES = (12, 16, 23, 32, 46, 64, 91)


def passed_along(block, axis, distance):
    devices = range(lax.axis_size(axis))
    route = [((i - distance) % len(devices), i) for i in devices]
    return lax.ppermute(block, axis, route)


def for_sending(value):

    def short(part):
        return part.astype(jnp.bfloat16) if part.dtype == jnp.float32 else part

    return jax.tree.map(short, value)


def bucket_index(offset):
    distance = jnp.abs(offset)
    far_bucket = 8 + sum(((distance >= edge).astype(jnp.int32) for edge in BUCKET_EDGES))
    near_or_far = jnp.where(distance < 8, distance, far_bucket)
    return near_or_far + jnp.where(offset > 0, 16, 0)


def rms_scale(values, gain_vector):
    return values * lax.rsqrt(jnp.mean(values * values, axis=-1, keepdims=True) + EPS) * gain_vector


def gelu_exact(values):
    return jax.nn.gelu(values, approximate=False)


def rows_product(left, right):
    return lax.dot_general(
        left, right, (((0,), (0,)), ((), ())), preferred_element_type=jnp.float32
    )


def times_transposed(left, right):
    return lax.dot_general(
        left, right, (((1,), (1,)), ((), ())), preferred_element_type=jnp.float32
    )


def move_keys(blocks):
    return (passed_along(blocks[0], "ctx", 1),)


def move_grads(blocks):
    return (passed_along(for_sending(blocks[0]), "ctx", 1),)


def on_device(
    inputs,
    teacher,
    seq_lengths,
    gain_attn,
    w_query,
    w_key,
    w_value,
    w_out,
    bias_table,
    gain_ffn,
    w_inner,
    w_outer,
):
    cycle_size = lax.axis_size("ctx")
    cycle_pos = lax.axis_index("ctx")
    token_total = SEQ_DEV * PIECE * cycle_size * lax.axis_size("wsh")
    row_count = SEQ_DEV * PIECE
    shards = (gain_attn, w_query, w_key, w_value, w_out, bias_table, gain_ffn, w_inner, w_outer)
    gathered = (
        lax.all_gather(shards[0], "wsh", axis=0, tiled=True),
        lax.all_gather(shards[1], "wsh", axis=0, tiled=True),
        lax.all_gather(shards[2], "wsh", axis=0, tiled=True),
        lax.all_gather(shards[3], "wsh", axis=0, tiled=True),
        lax.all_gather(shards[4], "wsh", axis=0, tiled=True),
        lax.all_gather(shards[5], "wsh", axis=0, tiled=True),
        lax.all_gather(shards[6], "wsh", axis=0, tiled=True),
        lax.all_gather(shards[7], "wsh", axis=0, tiled=True),
        lax.all_gather(shards[8], "wsh", axis=0, tiled=True),
    )
    (
        attn_gain,
        query_full,
        key_full,
        value_full,
        out_full,
        table_full,
        ffn_gain,
        inner_full,
        outer_full,
    ) = gathered
    lane_plans = ((0, H, 1),)
    x_rows = inputs.reshape(row_count, D).astype(jnp.float32)
    normed, attn_norm_back = jax.vjp(rms_scale, x_rows, attn_gain.astype(jnp.float32))
    normed_low = normed.astype(jnp.bfloat16)
    query_low = jnp.dot(normed_low, query_full, preferred_element_type=jnp.float32).astype(
        jnp.bfloat16
    )
    key_low = jnp.dot(normed_low, key_full, preferred_element_type=jnp.float32).astype(jnp.bfloat16)
    value_low = jnp.dot(normed_low, value_full, preferred_element_type=jnp.float32).astype(
        jnp.bfloat16
    )
    query_heads = query_low.reshape(SEQ_DEV, PIECE, H, DH)
    key_value = jnp.stack([key_low, value_low]).reshape(2, SEQ_DEV, PIECE, H * DH)
    places = jnp.arange(PIECE, dtype=jnp.int32)
    query_places = cycle_pos * PIECE + places
    bucket_ids = jnp.arange(BUCKETS, dtype=jnp.int32)

    def lane_blocks(stacked):
        return tuple((stacked for plan in lane_plans))

    def lane_scores(lane_plan, query_part, lane_block, key_start, table_rows):
        head_count = lane_plan[1] - lane_plan[0]
        key_count = lane_block.shape[2]
        key_places = key_start + jnp.arange(key_count, dtype=jnp.int32)
        offset = (key_places[None, :] - query_places[:, None]).reshape(-1)
        onehot = (bucket_index(offset)[None, :] == bucket_ids[:, None]).astype(jnp.bfloat16)
        bias_rows = jnp.dot(table_rows, onehot, preferred_element_type=jnp.float32)
        key_part = lane_block[0].reshape(SEQ_DEV, key_count, head_count, DH)
        scores = jnp.einsum(
            "sihd,sjhd->shij", query_part, key_part, preferred_element_type=jnp.float32
        )
        scores = scores + bias_rows.reshape(head_count, PIECE, key_count)[None]
        key_ok = key_places[None, :] < seq_lengths[:, None]
        return (jnp.where(key_ok[:, None, None, :], scores, NEG_FILL), onehot)

    table_forward = table_full.T

    def absorb(lane_plan, lane_state, lane_block, key_start):
        head_count = lane_plan[1] - lane_plan[0]
        key_count = lane_block.shape[2]
        row_max, row_total, accum = lane_state
        scores, onehot = lane_scores(lane_plan, query_heads, lane_block, key_start, table_forward)
        new_max = jnp.maximum(row_max, jnp.max(scores, axis=-1))
        rescale = jnp.exp(row_max - new_max)
        weights = jnp.exp(scores - new_max[..., None])
        row_total = row_total * rescale + jnp.sum(weights, axis=-1)
        value_part = lane_block[1].reshape(SEQ_DEV, key_count, head_count, DH)
        update = jnp.einsum(
            "shij,sjhd->sihd",
            weights.astype(jnp.bfloat16),
            value_part,
            preferred_element_type=jnp.float32,
        )
        accum = accum * jnp.transpose(rescale, (0, 2, 1))[..., None] + update
        return (new_max, row_total, accum)

    def empty_state(plan):
        head_count = plan[1] - plan[0]
        return (
            jnp.full((SEQ_DEV, head_count, PIECE), NEG_FILL, jnp.float32),
            jnp.zeros((SEQ_DEV, head_count, PIECE), jnp.float32),
            jnp.zeros((SEQ_DEV, PIECE, head_count, DH), jnp.float32),
        )

    def empty_accum(plan):
        head_count = plan[1] - plan[0]
        return (
            jnp.zeros((SEQ_DEV, PIECE, head_count, DH), jnp.float32),
            jnp.zeros((head_count, BUCKETS), jnp.float32),
        )

    blocks = lane_blocks(key_value)
    states = tuple(
        (
            absorb(plan, empty_state(plan), lane_block, cycle_pos * PIECE)
            for plan, lane_block in zip(lane_plans, blocks)
        )
    )

    def forward_turn(turn_index, loop_carry):
        arrived = move_keys(loop_carry[0])
        new_states = tuple(
            (
                absorb(
                    plan,
                    lane_state,
                    lane_block,
                    (cycle_pos - plan[2] * turn_index) % cycle_size * PIECE,
                )
                for plan, lane_state, lane_block in zip(lane_plans, loop_carry[1], arrived)
            )
        )
        return (arrived, new_states)

    blocks, states = lax.fori_loop(1, cycle_size, forward_turn, (blocks, states))
    log_totals = jnp.concatenate(
        [lane_state[0] + jnp.log(lane_state[1]) for lane_state in states], axis=1
    )
    attn_out = jnp.concatenate(
        [
            lane_state[2] / jnp.transpose(lane_state[1], (0, 2, 1))[..., None]
            for lane_state in states
        ],
        axis=2,
    )
    attn_low = attn_out.reshape(row_count, H * DH).astype(jnp.bfloat16)
    hidden = x_rows + jnp.dot(attn_low, out_full, preferred_element_type=jnp.float32)
    normed_ffn, ffn_norm_back = jax.vjp(rms_scale, hidden, ffn_gain.astype(jnp.float32))
    ffn_low = normed_ffn.astype(jnp.bfloat16)
    inner_sum = jnp.dot(ffn_low, inner_full, preferred_element_type=jnp.float32)
    active, gelu_back = jax.vjp(gelu_exact, inner_sum)
    active_low = active.astype(jnp.bfloat16)
    result = hidden + jnp.dot(active_low, outer_full, preferred_element_type=jnp.float32)
    row_valid = (
        (query_places[None, :] < seq_lengths[:, None]).astype(jnp.float32).reshape(row_count, 1)
    )
    deviation = result - teacher.reshape(row_count, D).astype(jnp.float32)
    square_sum, valid_count = lax.psum(
        (jnp.sum(deviation * deviation * row_valid), jnp.sum(row_valid)), ("ctx", "wsh")
    )
    loss_value = square_sum / (valid_count * D)
    result_grad = token_total / valid_count * deviation * row_valid
    result_low = result_grad.astype(jnp.bfloat16)
    query_back = gathered[1]
    key_back = gathered[2]
    value_back = gathered[3]
    out_back = gathered[4]
    table_back = gathered[5].T
    inner_back = gathered[7]
    outer_back = gathered[8]
    outer_grad = rows_product(active_low, result_low)
    active_grad = times_transposed(result_low, outer_back)
    inner_grad = gelu_back(active_grad)[0].astype(jnp.bfloat16)
    inner_wgrad = rows_product(ffn_low, inner_grad)
    ffn_normed_grad = times_transposed(inner_grad, inner_back)
    hidden_part, ffn_gain_grad = ffn_norm_back(ffn_normed_grad)
    hidden_grad = result_grad + hidden_part
    hidden_low = hidden_grad.astype(jnp.bfloat16)
    out_wgrad = rows_product(attn_low, hidden_low)
    dout_heads = (
        times_transposed(hidden_low, out_back).astype(jnp.bfloat16).reshape(SEQ_DEV, PIECE, H, DH)
    )
    out_dot = jnp.transpose(jnp.sum(dout_heads.astype(jnp.float32) * attn_out, axis=-1), (0, 2, 1))

    def lane_back(lane_plan, lane_block, lane_accum, key_start):
        low_head, high_head = (lane_plan[0], lane_plan[1])
        head_count = high_head - low_head
        key_count = lane_block.shape[2]
        scores, onehot = lane_scores(lane_plan, query_heads, lane_block, key_start, table_back)
        probability = jnp.exp(scores - log_totals[:, low_head:high_head, :, None])
        prob_low = probability.astype(jnp.bfloat16)
        key_part = lane_block[0].reshape(SEQ_DEV, key_count, head_count, DH)
        value_part = lane_block[1].reshape(SEQ_DEV, key_count, head_count, DH)
        value_grad = jnp.einsum(
            "shij,sihd->sjhd", prob_low, dout_heads, preferred_element_type=jnp.float32
        )
        prob_grad = jnp.einsum(
            "sihd,sjhd->shij", dout_heads, value_part, preferred_element_type=jnp.float32
        )
        score_grad = (probability * (prob_grad - out_dot[:, low_head:high_head, :, None])).astype(
            jnp.bfloat16
        )
        query_grad = lane_accum[0] + jnp.einsum(
            "shij,sjhd->sihd", score_grad, key_part, preferred_element_type=jnp.float32
        )
        key_grad = jnp.einsum(
            "shij,sihd->sjhd", score_grad, query_heads, preferred_element_type=jnp.float32
        )
        table_grad = lane_accum[1] + jnp.einsum(
            "shk,bk->hb",
            score_grad.reshape(SEQ_DEV, head_count, PIECE * key_count),
            onehot,
            preferred_element_type=jnp.float32,
        )
        term = jnp.stack([key_grad, value_grad]).reshape(2, SEQ_DEV, key_count, head_count * DH)
        return (term, (query_grad, table_grad))

    blocks = lane_blocks(key_value)
    outcome = [
        lane_back(plan, lane_block, empty_accum(plan), cycle_pos * PIECE)
        for plan, lane_block in zip(lane_plans, blocks)
    ]
    grad_blocks = move_grads(tuple((entry[0] for entry in outcome)))
    accums = tuple((entry[1] for entry in outcome))

    def back_turn(turn_index, loop_carry):
        arrived = move_keys(loop_carry[0])
        outcome = [
            lane_back(
                plan,
                lane_block,
                lane_accum,
                (cycle_pos - plan[2] * turn_index) % cycle_size * PIECE,
            )
            for plan, lane_block, lane_accum in zip(lane_plans, arrived, loop_carry[2])
        ]
        new_grads = move_grads(
            tuple((grad_block + entry[0] for grad_block, entry in zip(loop_carry[1], outcome)))
        )
        return (arrived, new_grads, tuple((entry[1] for entry in outcome)))

    blocks, grad_blocks, accums = lax.fori_loop(
        1, cycle_size, back_turn, (blocks, grad_blocks, accums)
    )
    pair_grads = grad_blocks[0]
    query_grad_low = (
        jnp.concatenate([lane_accum[0] for lane_accum in accums], axis=2)
        .reshape(row_count, H * DH)
        .astype(jnp.bfloat16)
    )
    key_grad_low = pair_grads[0].reshape(row_count, H * DH).astype(jnp.bfloat16)
    value_grad_low = pair_grads[1].reshape(row_count, H * DH).astype(jnp.bfloat16)
    table_grad = jnp.concatenate([lane_accum[1] for lane_accum in accums], axis=0).T
    query_wgrad = rows_product(normed_low, query_grad_low)
    key_wgrad = rows_product(normed_low, key_grad_low)
    value_wgrad = rows_product(normed_low, value_grad_low)
    normed_grad = (
        times_transposed(query_grad_low, query_back)
        + times_transposed(key_grad_low, key_back)
        + times_transposed(value_grad_low, value_back)
    )
    input_part, attn_gain_grad = attn_norm_back(normed_grad)
    input_grad = hidden_grad + input_part
    local_grads = (
        attn_gain_grad,
        query_wgrad,
        key_wgrad,
        value_wgrad,
        out_wgrad,
        table_grad,
        ffn_gain_grad,
        inner_wgrad,
        outer_grad,
    )
    shares = (
        lax.psum_scatter(
            local_grads[0].astype(jnp.bfloat16), "wsh", scatter_dimension=0, tiled=True
        ).astype(jnp.float32),
        lax.psum_scatter(
            local_grads[1].astype(jnp.bfloat16), "wsh", scatter_dimension=0, tiled=True
        ).astype(jnp.float32),
        lax.psum_scatter(
            local_grads[2].astype(jnp.bfloat16), "wsh", scatter_dimension=0, tiled=True
        ).astype(jnp.float32),
        lax.psum_scatter(
            local_grads[3].astype(jnp.bfloat16), "wsh", scatter_dimension=0, tiled=True
        ).astype(jnp.float32),
        lax.psum_scatter(
            local_grads[4].astype(jnp.bfloat16), "wsh", scatter_dimension=0, tiled=True
        ).astype(jnp.float32),
        lax.psum_scatter(
            local_grads[5].astype(jnp.bfloat16), "wsh", scatter_dimension=0, tiled=True
        ).astype(jnp.float32),
        lax.psum_scatter(
            local_grads[6].astype(jnp.bfloat16), "wsh", scatter_dimension=0, tiled=True
        ).astype(jnp.float32),
        lax.psum_scatter(
            local_grads[7].astype(jnp.bfloat16), "wsh", scatter_dimension=0, tiled=True
        ).astype(jnp.float32),
        lax.psum_scatter(
            local_grads[8].astype(jnp.bfloat16), "wsh", scatter_dimension=0, tiled=True
        ).astype(jnp.float32),
    )
    totals = lax.psum(
        (
            shares[0],
            shares[1],
            shares[2],
            shares[3],
            shares[4],
            shares[5],
            shares[6],
            shares[7],
            shares[8],
        ),
        "ctx",
    )
    return (
        result.reshape(SEQ_DEV, PIECE, D).astype(jnp.bfloat16),
        loss_value,
        input_grad.reshape(SEQ_DEV, PIECE, D),
        totals[0],
        totals[1],
        totals[2],
        totals[3],
        totals[4],
        totals[5],
        totals[6],
        totals[7],
        totals[8],
    )


def solution(mesh):
    placed = (
        P("wsh", "ctx", None),
        P("wsh", "ctx", None),
        P("wsh"),
        P("wsh"),
        P("wsh", None),
        P("wsh", None),
        P("wsh", None),
        P("wsh", None),
        P("wsh", None),
        P("wsh"),
        P("wsh", None),
        P("wsh", None),
    )
    return jax.shard_map(
        on_device,
        mesh=mesh,
        in_specs=placed,
        out_specs=(
            P("wsh", "ctx", None),
            P(),
            P("wsh", "ctx", None),
            P("wsh"),
            P("wsh", None),
            P("wsh", None),
            P("wsh", None),
            P("wsh", None),
            P("wsh", None),
            P("wsh"),
            P("wsh", None),
            P("wsh", None),
        ),
        check_vma=False,
    )
```

profile of v0, /device:TPU:4, one launch (start us, length us, event | category | flops | bytes accessed | tf_op | source)
XLA Modules:
  0.0 1079.4 jit_solution(2276786720739246816)
XLA Ops:
  32.5 13.9 %all-gather.7.cloned.1.call-done = bf16[768,768]{1,0:T(8,128)(2,1)} async-done(((bf16[192,768]{1,0:T(8,128)(2,1)}), bf16[768,768]{1,0:T(8,128)(2,1)}) %all-gather.7.cloned.1.call-update) | async-done | bytes 1179664 | tf_op jit(solution)/shard_map/all_gather | solution.py:90
  51.4 14.1 %all-gather.9.cloned.1.call-done = bf16[768,768]{1,0:T(8,128)(2,1)} async-done(((bf16[192,768]{1,0:T(8,128)(2,1)}), bf16[768,768]{1,0:T(8,128)(2,1)}) %all-gather.9.cloned.1.call-update) | async-done | bytes 1179664 | tf_op jit(solution)/shard_map/all_gather | solution.py:91
  69.3 155.7 %while.44 = (s32[]{:T(128)}, bf16[2,2,128,768]{2,3,1,0:T(8,128)(2,1)}, f32[2,12,128]{2,1,0:T(8,128)S(1)}, f32[2,12,128]{2,1,0:T(8,128)}, f32[2,128,12,64]{1,3,2,...) while((s32[]{:T(128)}, ...), condition=%wide.region_6.7_spmd.clone, body=%wide.region_3.6_spmd.clone.sunk | while | flops 117384720 | bytes 21013696 | solution.py:203
  73.1 19.0 %collective-permute-done = bf16[2,2,128,768]{2,3,1,0:T(8,128)(2,1)S(1)} collective-permute-done((bf16[2,2,128,768]{2,3,1,0:T(8,128)(2,1)}, bf16[2,2,128,768]{2,3,1,0:T(8,128)(2,1)S(1)}, u32[]{:S(2)}, u32[]{:S(2)}) %collective-permute-start) | collective-permute-done | bytes 786464 | tf_op jit(solution)/shard_map/while/body/eval_jaxpr/ppermute | solution.py:22
  96.4 19.9 %collective-permute-done = bf16[2,2,128,768]{2,3,1,0:T(8,128)(2,1)S(1)} collective-permute-done((bf16[2,2,128,768]{2,3,1,0:T(8,128)(2,1)}, bf16[2,2,128,768]{2,3,1,0:T(8,128)(2,1)S(1)}, u32[]{:S(2)}, u32[]{:S(2)}) %collective-permute-start) | collective-permute-done | bytes 786464 | tf_op jit(solution)/shard_map/while/body/eval_jaxpr/ppermute | solution.py:22
  120.4 19.0 %collective-permute-done = bf16[2,2,128,768]{2,3,1,0:T(8,128)(2,1)S(1)} collective-permute-done((bf16[2,2,128,768]{2,3,1,0:T(8,128)(2,1)}, bf16[2,2,128,768]{2,3,1,0:T(8,128)(2,1)S(1)}, u32[]{:S(2)}, u32[]{:S(2)}) %collective-permute-start) | collective-permute-done | bytes 786464 | tf_op jit(solution)/shard_map/while/body/eval_jaxpr/ppermute | solution.py:22
  143.6 18.0 %collective-permute-done = bf16[2,2,128,768]{2,3,1,0:T(8,128)(2,1)S(1)} collective-permute-done((bf16[2,2,128,768]{2,3,1,0:T(8,128)(2,1)}, bf16[2,2,128,768]{2,3,1,0:T(8,128)(2,1)S(1)}, u32[]{:S(2)}, u32[]{:S(2)}) %collective-permute-start) | collective-permute-done | bytes 786464 | tf_op jit(solution)/shard_map/while/body/eval_jaxpr/ppermute | solution.py:22
  165.8 17.1 %collective-permute-done = bf16[2,2,128,768]{2,3,1,0:T(8,128)(2,1)S(1)} collective-permute-done((bf16[2,2,128,768]{2,3,1,0:T(8,128)(2,1)}, bf16[2,2,128,768]{2,3,1,0:T(8,128)(2,1)S(1)}, u32[]{:S(2)}, u32[]{:S(2)}) %collective-permute-start) | collective-permute-done | bytes 786464 | tf_op jit(solution)/shard_map/while/body/eval_jaxpr/ppermute | solution.py:22
  187.1 16.2 %collective-permute-done = bf16[2,2,128,768]{2,3,1,0:T(8,128)(2,1)S(1)} collective-permute-done((bf16[2,2,128,768]{2,3,1,0:T(8,128)(2,1)}, bf16[2,2,128,768]{2,3,1,0:T(8,128)(2,1)S(1)}, u32[]{:S(2)}, u32[]{:S(2)}) %collective-permute-start) | collective-permute-done | bytes 786464 | tf_op jit(solution)/shard_map/while/body/eval_jaxpr/ppermute | solution.py:22
  207.5 15.3 %collective-permute-done = bf16[2,2,128,768]{2,3,1,0:T(8,128)(2,1)S(1)} collective-permute-done((bf16[2,2,128,768]{2,3,1,0:T(8,128)(2,1)}, bf16[2,2,128,768]{2,3,1,0:T(8,128)(2,1)S(1)}, u32[]{:S(2)}, u32[]{:S(2)}) %collective-permute-start) | collective-permute-done | bytes 786464 | tf_op jit(solution)/shard_map/while/body/eval_jaxpr/ppermute | solution.py:22
  246.6 39.2 %all-reduce.5 = (f32[]{:T(128)}, f32[]{:T(128)}) all-reduce(f32[]{:T(128)} %get-tuple-element.886, f32[]{:T(128)} %get-tuple-element.855), channel_id=1, replica_groups=mesh['ctx'=8,'wsh'=4] {'ctx','wsh'}, use_global_device_ids=true, to_apply=%region_9.10 | all-reduce | flops 2 | bytes 16 | tf_op jit(solution)/shard_map/psum | solution.py:226
  312.5 15.2 %collective-permute-done.3 = bf16[2,2,128,768]{2,3,1,0:T(8,128)(2,1)S(1)} collective-permute-done((bf16[2,2,128,768]{2,3,1,0:T(8,128)(2,1)}, bf16[2,2,128,768]{2,3,1,0:T(8,128)(2,1)S(1)}, u32[]{:S(2)}, u32[]{:S(2)}) %collective-permute-start.3) | collective-permute-done | bytes 786464 | tf_op jit(solution)/shard_map/ppermute | solution.py:22
  327.7 281.2 %while.45 = (s32[]{:T(128)}, bf16[2,2,128,768]{2,3,1,0:T(8,128)(2,1)}, bf16[2,2,128,768]{2,3,1,0:T(8,128)(2,1)S(1)}, f32[2,128,12,64]{1,3,2,0:T(8,128)S(1)}, f32...) while((s32[]{:T(128)}, ...), condition=%wide.region_17.18_spmd.clone, body=%wide.region_15.17_spmd.clone.sunk | while | flops 283444096 | bytes 33844516 | solution.py:310
  329.6 17.9 %collective-permute-done.1 = bf16[2,2,128,768]{2,3,1,0:T(8,128)(2,1)S(1)} collective-permute-done((bf16[2,2,128,768]{2,3,1,0:T(8,128)(2,1)}, bf16[2,2,128,768]{2,3,1,0:T(8,128)(2,1)S(1)}, u32[]{:S(2)}, u32[]{:S(2)}) %collective-permute-start.1) | collective-permute-done | bytes 786464 | tf_op jit(solution)/shard_map/while/body/eval_jaxpr/ppermute | solution.py:22
  352.5 15.9 %collective-permute-done.2 = bf16[2,2,128,768]{2,3,1,0:T(8,128)(2,1)S(1)} collective-permute-done((bf16[2,2,128,768]{2,3,1,0:T(8,128)(2,1)S(1)}, bf16[2,2,128,768]{2,3,1,0:T(8,128)(2,1)S(1)}, u32[]{:S(2)}, u32[]{:S(2)}) %collective-permute-start.2) | collective-permute-done | bytes 786464 | tf_op jit(solution)/shard_map/while/body/eval_jaxpr/ppermute | solution.py:22
  370.1 16.1 %collective-permute-done.1 = bf16[2,2,128,768]{2,3,1,0:T(8,128)(2,1)S(1)} collective-permute-done((bf16[2,2,128,768]{2,3,1,0:T(8,128)(2,1)}, bf16[2,2,128,768]{2,3,1,0:T(8,128)(2,1)S(1)}, u32[]{:S(2)}, u32[]{:S(2)}) %collective-permute-start.1) | collective-permute-done | bytes 786464 | tf_op jit(solution)/shard_map/while/body/eval_jaxpr/ppermute | solution.py:22
  391.2 15.0 %collective-permute-done.2 = bf16[2,2,128,768]{2,3,1,0:T(8,128)(2,1)S(1)} collective-permute-done((bf16[2,2,128,768]{2,3,1,0:T(8,128)(2,1)S(1)}, bf16[2,2,128,768]{2,3,1,0:T(8,128)(2,1)S(1)}, u32[]{:S(2)}, u32[]{:S(2)}) %collective-permute-start.2) | collective-permute-done | bytes 786464 | tf_op jit(solution)/shard_map/while/body/eval_jaxpr/ppermute | solution.py:22
  407.9 14.3 %collective-permute-done.1 = bf16[2,2,128,768]{2,3,1,0:T(8,128)(2,1)S(1)} collective-permute-done((bf16[2,2,128,768]{2,3,1,0:T(8,128)(2,1)}, bf16[2,2,128,768]{2,3,1,0:T(8,128)(2,1)S(1)}, u32[]{:S(2)}, u32[]{:S(2)}) %collective-permute-start.1) | collective-permute-done | bytes 786464 | tf_op jit(solution)/shard_map/while/body/eval_jaxpr/ppermute | solution.py:22
  427.2 15.0 %collective-permute-done.2 = bf16[2,2,128,768]{2,3,1,0:T(8,128)(2,1)S(1)} collective-permute-done((bf16[2,2,128,768]{2,3,1,0:T(8,128)(2,1)S(1)}, bf16[2,2,128,768]{2,3,1,0:T(8,128)(2,1)S(1)}, u32[]{:S(2)}, u32[]{:S(2)}) %collective-permute-start.2) | collective-permute-done | bytes 786464 | tf_op jit(solution)/shard_map/while/body/eval_jaxpr/ppermute | solution.py:22
  443.9 14.7 %collective-permute-done.1 = bf16[2,2,128,768]{2,3,1,0:T(8,128)(2,1)S(1)} collective-permute-done((bf16[2,2,128,768]{2,3,1,0:T(8,128)(2,1)}, bf16[2,2,128,768]{2,3,1,0:T(8,128)(2,1)S(1)}, u32[]{:S(2)}, u32[]{:S(2)}) %collective-permute-start.1) | collective-permute-done | bytes 786464 | tf_op jit(solution)/shard_map/while/body/eval_jaxpr/ppermute | solution.py:22
  463.6 17.0 %collective-permute-done.2 = bf16[2,2,128,768]{2,3,1,0:T(8,128)(2,1)S(1)} collective-permute-done((bf16[2,2,128,768]{2,3,1,0:T(8,128)(2,1)S(1)}, bf16[2,2,128,768]{2,3,1,0:T(8,128)(2,1)S(1)}, u32[]{:S(2)}, u32[]{:S(2)}) %collective-permute-start.2) | collective-permute-done | bytes 786464 | tf_op jit(solution)/shard_map/while/body/eval_jaxpr/ppermute | solution.py:22
  482.3 16.9 %collective-permute-done.1 = bf16[2,2,128,768]{2,3,1,0:T(8,128)(2,1)S(1)} collective-permute-done((bf16[2,2,128,768]{2,3,1,0:T(8,128)(2,1)}, bf16[2,2,128,768]{2,3,1,0:T(8,128)(2,1)S(1)}, u32[]{:S(2)}, u32[]{:S(2)}) %collective-permute-start.1) | collective-permute-done | bytes 786464 | tf_op jit(solution)/shard_map/while/body/eval_jaxpr/ppermute | solution.py:22
  504.2 19.2 %collective-permute-done.2 = bf16[2,2,128,768]{2,3,1,0:T(8,128)(2,1)S(1)} collective-permute-done((bf16[2,2,128,768]{2,3,1,0:T(8,128)(2,1)S(1)}, bf16[2,2,128,768]{2,3,1,0:T(8,128)(2,1)S(1)}, u32[]{:S(2)}, u32[]{:S(2)}) %collective-permute-start.2) | collective-permute-done | bytes 786464 | tf_op jit(solution)/shard_map/while/body/eval_jaxpr/ppermute | solution.py:22
  525.1 19.1 %collective-permute-done.1 = bf16[2,2,128,768]{2,3,1,0:T(8,128)(2,1)S(1)} collective-permute-done((bf16[2,2,128,768]{2,3,1,0:T(8,128)(2,1)}, bf16[2,2,128,768]{2,3,1,0:T(8,128)(2,1)S(1)}, u32[]{:S(2)}, u32[]{:S(2)}) %collective-permute-start.1) | collective-permute-done | bytes 786464 | tf_op jit(solution)/shard_map/while/body/eval_jaxpr/ppermute | solution.py:22
  549.1 19.8 %collective-permute-done.2 = bf16[2,2,128,768]{2,3,1,0:T(8,128)(2,1)S(1)} collective-permute-done((bf16[2,2,128,768]{2,3,1,0:T(8,128)(2,1)S(1)}, bf16[2,2,128,768]{2,3,1,0:T(8,128)(2,1)S(1)}, u32[]{:S(2)}, u32[]{:S(2)}) %collective-permute-start.2) | collective-permute-done | bytes 786464 | tf_op jit(solution)/shard_map/while/body/eval_jaxpr/ppermute | solution.py:22
  570.6 21.1 %collective-permute-done.1 = bf16[2,2,128,768]{2,3,1,0:T(8,128)(2,1)S(1)} collective-permute-done((bf16[2,2,128,768]{2,3,1,0:T(8,128)(2,1)}, bf16[2,2,128,768]{2,3,1,0:T(8,128)(2,1)S(1)}, u32[]{:S(2)}, u32[]{:S(2)}) %collective-permute-start.1) | collective-permute-done | bytes 786464 | tf_op jit(solution)/shard_map/while/body/eval_jaxpr/ppermute | solution.py:22
  596.7 12.2 %collective-permute-done.2 = bf16[2,2,128,768]{2,3,1,0:T(8,128)(2,1)S(1)} collective-permute-done((bf16[2,2,128,768]{2,3,1,0:T(8,128)(2,1)S(1)}, bf16[2,2,128,768]{2,3,1,0:T(8,128)(2,1)S(1)}, u32[]{:S(2)}, u32[]{:S(2)}) %collective-permute-start.2) | collective-permute-done | bytes 786464 | tf_op jit(solution)/shard_map/while/body/eval_jaxpr/ppermute | solution.py:22
  642.8 19.1 %reduce-scatter.11.cloned.1.call-done = bf16[192,768]{1,0:T(8,128)(2,1)} async-done(((bf16[768,768]{1,0:T(8,128)(2,1)}), bf16[192,768]{1,0:T(8,128)(2,1)}) %reduce-scatter.11.cloned.1.call-update) | async-done | bytes 294928 | tf_op jit(solution)/shard_map/reduce_scatter | solution.py:353
  661.9 28.9 %reduce-scatter.7.cloned.1.call-done = bf16[192,768]{1,0:T(8,128)(2,1)} async-done(((bf16[768,768]{1,0:T(8,128)(2,1)}), bf16[192,768]{1,0:T(8,128)(2,1)}) %reduce-scatter.7.cloned.1.call-update) | async-done | bytes 294928 | tf_op jit(solution)/shard_map/reduce_scatter | solution.py:347
  690.8 50.4 %reduce-scatter.15.cloned.1.call-done = bf16[192,3072]{1,0:T(8,128)(2,1)} async-done(((bf16[768,3072]{1,0:T(8,128)(2,1)}), bf16[192,3072]{1,0:T(8,128)(2,1)}) %reduce-scatter.15.cloned.1.call-update) | async-done | bytes 1179664 | tf_op jit(solution)/shard_map/reduce_scatter | solution.py:365
  741.2 50.5 %reduce-scatter.17.cloned.1.call-done = bf16[768,768]{1,0:T(8,128)(2,1)} async-done(((bf16[3072,768]{1,0:T(8,128)(2,1)}), bf16[768,768]{1,0:T(8,128)(2,1)}) %reduce-scatter.17.cloned.1.call-update) | async-done | bytes 1179664 | tf_op jit(solution)/shard_map/reduce_scatter | solution.py:368
  791.7 279.3 %all-reduce.10 = (f32[192]{0:T(256)}, f32[192,768]{1,0:T(8,128)}, f32[192,768]{1,0:T(8,128)}, f32[192,768]{1,0:T(8,128)}, f32[192,768]{1,0:T(8,128)}, /*index=5*...) all-reduce(f32[192]{0:T(256)S(1)} %get-tuple-element.893, ...), channel_id=1, replica_groups=mesh['ctx'=8,'wsh'=4] {'ctx'}, use_global_device_ids=true, to_apply=%region_21.22 | all-reduce | flops 1769952 | bytes 10620672 | tf_op jit(solution)/shard_map/psum | solution.py:372
  (604 shorter events, 186.7 us)
Async XLA Ops:
  7.2 23.2 %all-gather.11.cloned.1.call-start = ((), (), s32[]{:S(2)}) async-start(), calls=%async_computation.8 | async-start | bytes 1474560 | tf_op jit(solution)/shard_map/all_gather | solution.py:89
  8.0 38.4 %all-gather.7.cloned.1.call-start = ((), (), s32[]{:S(2)}) async-start(), calls=%async_computation.6 | async-start | bytes 1474560 | tf_op jit(solution)/shard_map/all_gather | solution.py:90
  8.7 56.7 %all-gather.9.cloned.1.call-start = ((), (), s32[]{:S(2)}) async-start(), calls=%async_computation.7 | async-start | bytes 1474560 | tf_op jit(solution)/shard_map/all_gather | solution.py:91
  9.5 218.0 %all-gather.13.cloned.1.call-start = ((), (), s32[]{:S(2)}) async-start(), calls=%async_computation.9 | async-start | bytes 1474560 | tf_op jit(solution)/shard_map/all_gather | solution.py:92
  10.0 220.3 %all-gather.15.cloned.1.call-start = ((), (), s32[]{:S(2)}) async-start(), calls=%async_computation.10 | async-start | bytes 5898240 | tf_op jit(solution)/shard_map/all_gather | solution.py:95
  10.6 230.9 %all-gather.17.cloned.1.call-start = ((), (), s32[]{:S(2)}) async-start(), calls=%async_computation.11 | async-start | bytes 5898240 | tf_op jit(solution)/shard_map/all_gather | solution.py:96
  11.2 631.6 %reduce-scatter.13.cloned.1.call-start = ((), (), s32[]{:S(2)}) async-start(), calls=%async_computation.15 | async-start | bytes 1474560 | tf_op jit(solution)/shard_map/reduce_scatter | solution.py:356
  69.5 22.7 %collective-permute-start = (bf16[2,2,128,768]{2,3,1,0:T(8,128)(2,1)}, bf16[2,2,128,768]{2,3,1,0:T(8,128)(2,1)S(1)}, u32[]{:S(2)}, u32[]{:S(2)}) collective-permute-start(bf16[2,2,128,768]{2,3,1,0:T(8,128)(2,1)} %get-tuple-element.1078), channel_id=1, source_target_pairs={{28,0},{0,4},{4,8},{8,12},{12,16},{16,20},{20,24},{24,28},{29,1},{... | collective-permute-start | bytes 2359304 | tf_op jit(solution)/shard_map/while/body/eval_jaxpr/ppermute | solution.py:22
  94.4 21.8 %collective-permute-start = (bf16[2,2,128,768]{2,3,1,0:T(8,128)(2,1)}, bf16[2,2,128,768]{2,3,1,0:T(8,128)(2,1)S(1)}, u32[]{:S(2)}, u32[]{:S(2)}) collective-permute-start(bf16[2,2,128,768]{2,3,1,0:T(8,128)(2,1)} %get-tuple-element.1078), channel_id=1, source_target_pairs={{28,0},{0,4},{4,8},{8,12},{12,16},{16,20},{20,24},{24,28},{29,1},{... | collective-permute-start | bytes 2359304 | tf_op jit(solution)/shard_map/while/body/eval_jaxpr/ppermute | solution.py:22
  118.5 20.9 %collective-permute-start = (bf16[2,2,128,768]{2,3,1,0:T(8,128)(2,1)}, bf16[2,2,128,768]{2,3,1,0:T(8,128)(2,1)S(1)}, u32[]{:S(2)}, u32[]{:S(2)}) collective-permute-start(bf16[2,2,128,768]{2,3,1,0:T(8,128)(2,1)} %get-tuple-element.1078), channel_id=1, source_target_pairs={{28,0},{0,4},{4,8},{8,12},{12,16},{16,20},{20,24},{24,28},{29,1},{... | collective-permute-start | bytes 2359304 | tf_op jit(solution)/shard_map/while/body/eval_jaxpr/ppermute | solution.py:22
  141.7 20.0 %collective-permute-start = (bf16[2,2,128,768]{2,3,1,0:T(8,128)(2,1)}, bf16[2,2,128,768]{2,3,1,0:T(8,128)(2,1)S(1)}, u32[]{:S(2)}, u32[]{:S(2)}) collective-permute-start(bf16[2,2,128,768]{2,3,1,0:T(8,128)(2,1)} %get-tuple-element.1078), channel_id=1, source_target_pairs={{28,0},{0,4},{4,8},{8,12},{12,16},{16,20},{20,24},{24,28},{29,1},{... | collective-permute-start | bytes 2359304 | tf_op jit(solution)/shard_map/while/body/eval_jaxpr/ppermute | solution.py:22
  163.9 19.0 %collective-permute-start = (bf16[2,2,128,768]{2,3,1,0:T(8,128)(2,1)}, bf16[2,2,128,768]{2,3,1,0:T(8,128)(2,1)S(1)}, u32[]{:S(2)}, u32[]{:S(2)}) collective-permute-start(bf16[2,2,128,768]{2,3,1,0:T(8,128)(2,1)} %get-tuple-element.1078), channel_id=1, source_target_pairs={{28,0},{0,4},{4,8},{8,12},{12,16},{16,20},{20,24},{24,28},{29,1},{... | collective-permute-start | bytes 2359304 | tf_op jit(solution)/shard_map/while/body/eval_jaxpr/ppermute | solution.py:22
  185.2 18.1 %collective-permute-start = (bf16[2,2,128,768]{2,3,1,0:T(8,128)(2,1)}, bf16[2,2,128,768]{2,3,1,0:T(8,128)(2,1)S(1)}, u32[]{:S(2)}, u32[]{:S(2)}) collective-permute-start(bf16[2,2,128,768]{2,3,1,0:T(8,128)(2,1)} %get-tuple-element.1078), channel_id=1, source_target_pairs={{28,0},{0,4},{4,8},{8,12},{12,16},{16,20},{20,24},{24,28},{29,1},{... | collective-permute-start | bytes 2359304 | tf_op jit(solution)/shard_map/while/body/eval_jaxpr/ppermute | solution.py:22
  205.6 17.2 %collective-permute-start = (bf16[2,2,128,768]{2,3,1,0:T(8,128)(2,1)}, bf16[2,2,128,768]{2,3,1,0:T(8,128)(2,1)S(1)}, u32[]{:S(2)}, u32[]{:S(2)}) collective-permute-start(bf16[2,2,128,768]{2,3,1,0:T(8,128)(2,1)} %get-tuple-element.1078), channel_id=1, source_target_pairs={{28,0},{0,4},{4,8},{8,12},{12,16},{16,20},{20,24},{24,28},{29,1},{... | collective-permute-start | bytes 2359304 | tf_op jit(solution)/shard_map/while/body/eval_jaxpr/ppermute | solution.py:22
  307.2 20.5 %collective-permute-start.3 = (bf16[2,2,128,768]{2,3,1,0:T(8,128)(2,1)}, bf16[2,2,128,768]{2,3,1,0:T(8,128)(2,1)S(1)}, u32[]{:S(2)}, u32[]{:S(2)}) collective-permute-start(bf16[2,2,128,768]{2,3,1,0:T(8,128)(2,1)} %pad_maximum_fusion.1), channel_id=1, source_target_pairs={{28,0},{0,4},{4,8},{8,12},{12,16},{16,20},{20,24},{24,28},{29,1},{... | collective-permute-start | bytes 2359304 | tf_op jit(solution)/shard_map/ppermute | solution.py:22
  309.3 333.5 %reduce-scatter.9.cloned.1.call-start = ((), (), s32[]{:S(2)}) async-start(), calls=%async_computation.13 | async-start | bytes 1474560 | tf_op jit(solution)/shard_map/reduce_scatter | solution.py:350
  327.9 19.6 %collective-permute-start.1 = (bf16[2,2,128,768]{2,3,1,0:T(8,128)(2,1)}, bf16[2,2,128,768]{2,3,1,0:T(8,128)(2,1)S(1)}, u32[]{:S(2)}, u32[]{:S(2)}) collective-permute-start(bf16[2,2,128,768]{2,3,1,0:T(8,128)(2,1)} %get-tuple-element.1127), channel_id=1, source_target_pairs={{28,0},{0,4},{4,8},{8,12},{12,16},{16,20},{20,24},{24,28},{29,1},{... | collective-permute-start | bytes 2359304 | tf_op jit(solution)/shard_map/while/body/eval_jaxpr/ppermute | solution.py:22
  350.0 18.5 %collective-permute-start.2 = (bf16[2,2,128,768]{2,3,1,0:T(8,128)(2,1)S(1)}, bf16[2,2,128,768]{2,3,1,0:T(8,128)(2,1)S(1)}, u32[]{:S(2)}, u32[]{:S(2)}) collective-permute-start(bf16[2,2,128,768]{2,3,1,0:T(8,128)(2,1)S(1)} %fusion.222), channel_id=1, source_target_pairs={{28,0},{0,4},{4,8},{8,12},{12,16},{16,20},{20,24},{24,28},{29,1},{... | collective-permute-start | bytes 2359304 | tf_op jit(solution)/shard_map/while/body/eval_jaxpr/ppermute | solution.py:22
  368.5 17.7 %collective-permute-start.1 = (bf16[2,2,128,768]{2,3,1,0:T(8,128)(2,1)}, bf16[2,2,128,768]{2,3,1,0:T(8,128)(2,1)S(1)}, u32[]{:S(2)}, u32[]{:S(2)}) collective-permute-start(bf16[2,2,128,768]{2,3,1,0:T(8,128)(2,1)} %get-tuple-element.1127), channel_id=1, source_target_pairs={{28,0},{0,4},{4,8},{8,12},{12,16},{16,20},{20,24},{24,28},{29,1},{... | collective-permute-start | bytes 2359304 | tf_op jit(solution)/shard_map/while/body/eval_jaxpr/ppermute | solution.py:22
  388.7 17.5 %collective-permute-start.2 = (bf16[2,2,128,768]{2,3,1,0:T(8,128)(2,1)S(1)}, bf16[2,2,128,768]{2,3,1,0:T(8,128)(2,1)S(1)}, u32[]{:S(2)}, u32[]{:S(2)}) collective-permute-start(bf16[2,2,128,768]{2,3,1,0:T(8,128)(2,1)S(1)} %fusion.222), channel_id=1, source_target_pairs={{28,0},{0,4},{4,8},{8,12},{12,16},{16,20},{20,24},{24,28},{29,1},{... | collective-permute-start | bytes 2359304 | tf_op jit(solution)/shard_map/while/body/eval_jaxpr/ppermute | solution.py:22
  424.7 17.5 %collective-permute-start.2 = (bf16[2,2,128,768]{2,3,1,0:T(8,128)(2,1)S(1)}, bf16[2,2,128,768]{2,3,1,0:T(8,128)(2,1)S(1)}, u32[]{:S(2)}, u32[]{:S(2)}) collective-permute-start(bf16[2,2,128,768]{2,3,1,0:T(8,128)(2,1)S(1)} %fusion.222), channel_id=1, source_target_pairs={{28,0},{0,4},{4,8},{8,12},{12,16},{16,20},{20,24},{24,28},{29,1},{... | collective-permute-start | bytes 2359304 | tf_op jit(solution)/shard_map/while/body/eval_jaxpr/ppermute | solution.py:22
  442.2 16.4 %collective-permute-start.1 = (bf16[2,2,128,768]{2,3,1,0:T(8,128)(2,1)}, bf16[2,2,128,768]{2,3,1,0:T(8,128)(2,1)S(1)}, u32[]{:S(2)}, u32[]{:S(2)}) collective-permute-start(bf16[2,2,128,768]{2,3,1,0:T(8,128)(2,1)} %get-tuple-element.1127), channel_id=1, source_target_pairs={{28,0},{0,4},{4,8},{8,12},{12,16},{16,20},{20,24},{24,28},{29,1},{... | collective-permute-start | bytes 2359304 | tf_op jit(solution)/shard_map/while/body/eval_jaxpr/ppermute | solution.py:22
  461.1 19.6 %collective-permute-start.2 = (bf16[2,2,128,768]{2,3,1,0:T(8,128)(2,1)S(1)}, bf16[2,2,128,768]{2,3,1,0:T(8,128)(2,1)S(1)}, u32[]{:S(2)}, u32[]{:S(2)}) collective-permute-start(bf16[2,2,128,768]{2,3,1,0:T(8,128)(2,1)S(1)} %fusion.222), channel_id=1, source_target_pairs={{28,0},{0,4},{4,8},{8,12},{12,16},{16,20},{20,24},{24,28},{29,1},{... | collective-permute-start | bytes 2359304 | tf_op jit(solution)/shard_map/while/body/eval_jaxpr/ppermute | solution.py:22
  480.6 18.5 %collective-permute-start.1 = (bf16[2,2,128,768]{2,3,1,0:T(8,128)(2,1)}, bf16[2,2,128,768]{2,3,1,0:T(8,128)(2,1)S(1)}, u32[]{:S(2)}, u32[]{:S(2)}) collective-permute-start(bf16[2,2,128,768]{2,3,1,0:T(8,128)(2,1)} %get-tuple-element.1127), channel_id=1, source_target_pairs={{28,0},{0,4},{4,8},{8,12},{12,16},{16,20},{20,24},{24,28},{29,1},{... | collective-permute-start | bytes 2359304 | tf_op jit(solution)/shard_map/while/body/eval_jaxpr/ppermute | solution.py:22
  501.6 21.8 %collective-permute-start.2 = (bf16[2,2,128,768]{2,3,1,0:T(8,128)(2,1)S(1)}, bf16[2,2,128,768]{2,3,1,0:T(8,128)(2,1)S(1)}, u32[]{:S(2)}, u32[]{:S(2)}) collective-permute-start(bf16[2,2,128,768]{2,3,1,0:T(8,128)(2,1)S(1)} %fusion.222), channel_id=1, source_target_pairs={{28,0},{0,4},{4,8},{8,12},{12,16},{16,20},{20,24},{24,28},{29,1},{... | collective-permute-start | bytes 2359304 | tf_op jit(solution)/shard_map/while/body/eval_jaxpr/ppermute | solution.py:22
  523.4 20.7 %collective-permute-start.1 = (bf16[2,2,128,768]{2,3,1,0:T(8,128)(2,1)}, bf16[2,2,128,768]{2,3,1,0:T(8,128)(2,1)S(1)}, u32[]{:S(2)}, u32[]{:S(2)}) collective-permute-start(bf16[2,2,128,768]{2,3,1,0:T(8,128)(2,1)} %get-tuple-element.1127), channel_id=1, source_target_pairs={{28,0},{0,4},{4,8},{8,12},{12,16},{16,20},{20,24},{24,28},{29,1},{... | collective-permute-start | bytes 2359304 | tf_op jit(solution)/shard_map/while/body/eval_jaxpr/ppermute | solution.py:22
  546.6 22.3 %collective-permute-start.2 = (bf16[2,2,128,768]{2,3,1,0:T(8,128)(2,1)S(1)}, bf16[2,2,128,768]{2,3,1,0:T(8,128)(2,1)S(1)}, u32[]{:S(2)}, u32[]{:S(2)}) collective-permute-start(bf16[2,2,128,768]{2,3,1,0:T(8,128)(2,1)S(1)} %fusion.222), channel_id=1, source_target_pairs={{28,0},{0,4},{4,8},{8,12},{12,16},{16,20},{20,24},{24,28},{29,1},{... | collective-permute-start | bytes 2359304 | tf_op jit(solution)/shard_map/while/body/eval_jaxpr/ppermute | solution.py:22
  568.9 22.7 %collective-permute-start.1 = (bf16[2,2,128,768]{2,3,1,0:T(8,128)(2,1)}, bf16[2,2,128,768]{2,3,1,0:T(8,128)(2,1)S(1)}, u32[]{:S(2)}, u32[]{:S(2)}) collective-permute-start(bf16[2,2,128,768]{2,3,1,0:T(8,128)(2,1)} %get-tuple-element.1127), channel_id=1, source_target_pairs={{28,0},{0,4},{4,8},{8,12},{12,16},{16,20},{20,24},{24,28},{29,1},{... | collective-permute-start | bytes 2359304 | tf_op jit(solution)/shard_map/while/body/eval_jaxpr/ppermute | solution.py:22
  611.5 50.4 %reduce-scatter.11.cloned.1.call-start = ((), (), s32[]{:S(2)}) async-start(), calls=%async_computation.14 | async-start | bytes 1474560 | tf_op jit(solution)/shard_map/reduce_scatter | solution.py:353
  613.1 77.7 %reduce-scatter.7.cloned.1.call-start = ((), (), s32[]{:S(2)}) async-start(), calls=%async_computation.12 | async-start | bytes 1474560 | tf_op jit(solution)/shard_map/reduce_scatter | solution.py:347
  615.3 125.9 %reduce-scatter.15.cloned.1.call-start = ((), (), s32[]{:S(2)}) async-start(), calls=%async_computation.16 | async-start | bytes 5898240 | tf_op jit(solution)/shard_map/reduce_scatter | solution.py:365
  620.6 171.1 %reduce-scatter.17.cloned.1.call-start = ((), (), s32[]{:S(2)}) async-start(), calls=%async_computation.17 | async-start | bytes 5898240 | tf_op jit(solution)/shard_map/reduce_scatter | solution.py:368
  (121 other events, 613.3 us)
Sparse Core Ops, SparseCore 0:
  9.6 17.5 all-gather.10
  28.8 17.5 all-gather.6
  47.9 17.4 all-gather.8
  66.8 17.4 all-gather.12
  85.7 37.4 all-gather.14
  124.6 37.4 all-gather.16
  309.4 25.3 reduce-scatter.12
  611.6 21.8 reduce-scatter.8
  636.0 25.8 reduce-scatter.10
  665.1 25.7 reduce-scatter.6
  693.3 47.8 reduce-scatter.14
  743.8 47.8 reduce-scatter.16
where the time goes:
time: 1090 us; the launch traced here: 1080 us
  waiting for transfers between devices  555 us (51%)
  blocking collectives  340 us (31%)
  matrix products  97.1 us (9%)
  local copies, waits for them, and re-layouts  35.9 us (3%)
  other arithmetic  25.6 us (2%)
  between operations  20.9 us (2%)
    ppermute x22, waiting for transfers between devices, passed_along(): return lax.ppermute(block, axis, route)  374 us
    psum x1, blocking collectives, on_device(): lax.psum((shares[0], shares[1], shares[2], shares[3], shares[4], shares[5...  279 us
    reduce_scatter x1, waiting for transfers between devices, on_device(): lax.psum_scatter(local_grads[8].astype(jnp.bfloat16), 'wsh', scatter_dime...  50.5 us
    reduce_scatter x1, waiting for transfers between devices, on_device(): lax.psum_scatter(local_grads[7].astype(jnp.bfloat16), 'wsh', scatter_dime...  50.4 us
    psum x1, blocking collectives, on_device(): lax.psum((jnp.sum(deviation * deviation * row_valid), jnp.sum(row_valid))...  39.2 us
    reduce_scatter x1, waiting for transfers between devices, on_device(): lax.psum_scatter(local_grads[1].astype(jnp.bfloat16), 'wsh', scatter_dime...  28.9 us
  transfers between devices with their start and end apart: 34, of which 28 were waited for; matrix products, arithmetic and copies ran while one was open for 12% of the time, Pallas kernels for 0%

commit v1 on v0

v1 whole, which is shorter than its diff:
```python
import functools

import jax
import jax.numpy as jnp
from jax import lax
from jax.experimental import pallas as pl
from jax.experimental.pallas import tpu as pltpu
from jax.sharding import PartitionSpec as P

D = 768
H = 12
DH = 64
BUCKETS = 32
SEQ_DEV = 2
PIECE = 128
TP = 4
HEADS = H // TP
COLS = HEADS * DH
ROWS = SEQ_DEV * PIECE
GROUP = ROWS * TP
EPS = 1e-06
NEG_FILL = -1e30
BUCKET_EDGES = (12, 16, 23, 32, 46, 64, 91)
AXES = ("ctx", "wsh")
ORDER = (0, 2, 1, 3)

BF16 = jnp.bfloat16
F32 = jnp.float32
NT = (((1,), (1,)), ((), ()))
TN = (((0,), (0,)), ((), ()))
NN = (((1,), (0,)), ((), ()))


def dot(left, right, dims=NN):
    return lax.dot_general(left, right, dims, preferred_element_type=F32)


def swapped(index):
    return (index & 1) * 2 + (index >> 1)


def seq_routes(n_ctx):
    spread = n_ctx // (SEQ_DEV * TP)
    same, cross = [], []
    for c in range(n_ctx):
        for w in range(TP):
            pair = c // 2
            for b in range(2):
                home = (2 * swapped(w) + b) * spread + pair // TP
                route = (c * TP + w, home * TP + swapped(pair % TP))
                (same if b == c % 2 else cross).append(route)
    return same, cross


def backwards(routes):
    return [(there, here) for here, there in routes]


def to_partner(value, offset):
    return lax.ppermute(value, "wsh", [(i, i ^ offset) for i in range(TP)])


def to_ctx(value, offset):
    n_ctx = lax.axis_size("ctx")
    return lax.ppermute(value, "ctx", [(i, i ^ offset) for i in range(n_ctx)])


def pick(stack, index):
    return lax.dynamic_index_in_dim(stack, index, 0, keepdims=False)


def by_owner(pieces, me):
    stack = jnp.stack(pieces)
    return jnp.stack([pick(stack, me ^ i) for i in range(len(pieces))])


def exchange_blocks(blocks, me):
    pieces = [pick(blocks, me)]
    for offset in range(1, TP):
        pieces.append(to_partner(pick(blocks, me ^ offset), offset))
    return by_owner(pieces, me)


def gather_group(value):
    from_y = to_partner(value, 2)
    core_own = to_partner(value, 1)
    core_y = to_partner(from_y, 1)
    return jnp.concatenate([value, from_y, core_own, core_y])


def scatter_group(keep, send):
    half = keep + to_partner(send, 1).astype(F32)
    other = half[ROWS:].astype(BF16)
    return half[:ROWS] + to_partner(other, 2).astype(F32)


def reduce_ctx(parts, ctx_me):
    n_ctx = lax.axis_size("ctx")
    if n_ctx != 8:
        return lax.psum_scatter(parts.astype(BF16), "ctx", scatter_dimension=0, tiled=False).astype(F32)
    x, z = ctx_me & 1, ctx_me >> 1
    halves = parts.reshape((4, 2) + parts.shape[1:])
    mine = lax.dynamic_index_in_dim(halves, x, 1, keepdims=False)
    other = lax.dynamic_index_in_dim(halves, 1 - x, 1, keepdims=False).astype(BF16)
    half = mine.astype(F32) + to_ctx(other, 1).astype(F32)
    total = pick(half, z)
    for offset in (1, 2, 3):
        total = total + to_ctx(pick(half, z ^ offset).astype(BF16), 2 * offset).astype(F32)
    return total


def gather_ctx(chunk, ctx_me):
    n_ctx = lax.axis_size("ctx")
    chunk = chunk.astype(BF16)
    if n_ctx != 8:
        return lax.all_gather(chunk, "ctx", axis=0, tiled=False)
    x, z = ctx_me & 1, ctx_me >> 1
    half = by_owner([chunk] + [to_ctx(chunk, 2 * offset) for offset in (1, 2, 3)], z)
    both = by_owner([half, to_ctx(half, 1)], x)
    return jnp.swapaxes(both, 0, 1).reshape((n_ctx,) + chunk.shape)


def bucket_index(offset):
    distance = jnp.abs(offset)
    far_bucket = 8 + sum(((distance >= edge).astype(jnp.int32) for edge in BUCKET_EDGES))
    near_or_far = jnp.where(distance < 8, distance, far_bucket)
    return near_or_far + jnp.where(offset > 0, 16, 0)


def gelu_and_slope(values):
    scaled = values * 0.7071067811865476
    cumulative = 0.5 * (1.0 + lax.erf(scaled))
    density = jnp.exp(-0.5 * values * values) * 0.3989422804014327
    return values * cumulative, cumulative + values * density


def repeat(count, unroll, body, carry):
    if unroll:
        for index in range(count):
            carry = body(index, carry)
        return carry
    return lax.fori_loop(0, count, body, carry)


def block_bias(bias_ref, places, head, key_block, query_block, blocks):
    tiles = []
    for i in range(blocks):
        apart = places[8 + key_block] - places[query_block + i]
        tiles.append(bias_ref[head, jnp.clip(apart, -2, 2) + 2])
    return tiles[0] if blocks == 1 else jnp.concatenate(tiles, axis=1)


def attention_kernel(
    chunk, offsets, places, q_ref, kv_ref, bias_ref, out_w_ref,
    keep_ref, send_ref, attn_ref, lse_ref, s_ref, p_ref,
):
    keys = kv_ref.shape[0]
    key_blocks = keys // PIECE
    length = places[8 + key_blocks]
    k_off, v_off = offsets
    blocks = chunk // PIECE
    unroll = key_blocks <= 8
    key_iota = lax.broadcasted_iota(jnp.int32, (PIECE, 1), 0)
    for head in range(HEADS):
        lanes = slice(head * DH, head * DH + DH)
        key_part = kv_ref[:, k_off + head * DH : k_off + head * DH + DH]
        value_part = kv_ref[:, v_off + head * DH : v_off + head * DH + DH]

        def for_queries(q_chunk, carry):
            rows = pl.ds(pl.multiple_of(q_chunk * chunk, chunk), chunk)
            s_ref[...] = dot(key_part, q_ref[rows, lanes], NT)

            def score(index, top):
                at = pl.ds(pl.multiple_of(index * PIECE, PIECE), PIECE)
                tile = s_ref[at, :] + block_bias(bias_ref, places, head, index, q_chunk * blocks, blocks)
                ok = places[8 + index] * PIECE + key_iota < length
                tile = jnp.where(ok, tile, NEG_FILL)
                s_ref[at, :] = tile
                return jnp.maximum(top, jnp.max(tile, axis=0, keepdims=True))

            top = repeat(key_blocks, unroll, score, jnp.full((1, chunk), NEG_FILL, F32))

            def weigh(index, total):
                at = pl.ds(pl.multiple_of(index * PIECE, PIECE), PIECE)
                weight = jnp.exp(s_ref[at, :] - top)
                p_ref[at, :] = weight.astype(BF16)
                return total + jnp.sum(weight, axis=0, keepdims=True)

            total = repeat(key_blocks, unroll, weigh, jnp.zeros((1, chunk), F32))
            attn_ref[lanes, rows] = dot(value_part, p_ref[...], TN) / total
            lse_ref[head : head + 1, rows] = top + jnp.log(total)
            return carry

        repeat(GROUP // chunk, unroll, for_queries, 0)
    partial = dot(attn_ref[...].astype(BF16), out_w_ref[...], TN)
    keep_ref[...] = partial[: GROUP // 2]
    send_ref[...] = partial[GROUP // 2 :].astype(BF16)


def attention_back_kernel(
    chunk, offsets, places, q_ref, kv_ref, bias_ref, out_w_ref, up_ref, attn_ref, lse_ref,
    dq_ref, dkv_ref, table_ref,
    s_ref, dp_ref, p_ref, ds_ref, do_ref, outdot_ref, dqt_ref, dkv_sum, tile_ref,
):
    keys = kv_ref.shape[0]
    key_blocks = keys // PIECE
    length = places[8 + key_blocks]
    k_off, v_off = offsets
    blocks = chunk // PIECE
    unroll = key_blocks <= 8
    key_iota = lax.broadcasted_iota(jnp.int32, (PIECE, 1), 0)
    do_ref[...] = dot(up_ref[...], out_w_ref[...], NT).astype(BF16)
    do_t = dot(out_w_ref[...], up_ref[...], NT).astype(BF16).astype(F32) * attn_ref[...]
    for head in range(HEADS):
        outdot_ref[head : head + 1, :] = jnp.sum(do_t[head * DH : head * DH + DH], axis=0, keepdims=True)
    tile_ref[...] = jnp.zeros_like(tile_ref)
    dkv_sum[...] = jnp.zeros_like(dkv_sum)
    for head in range(HEADS):
        lanes = slice(head * DH, head * DH + DH)
        key_part = kv_ref[:, k_off + head * DH : k_off + head * DH + DH]
        value_part = kv_ref[:, v_off + head * DH : v_off + head * DH + DH]

        def for_queries(q_chunk, carry):
            rows = pl.ds(pl.multiple_of(q_chunk * chunk, chunk), chunk)
            query_part = q_ref[rows, lanes]
            do_part = do_ref[rows, lanes]
            s_ref[...] = dot(key_part, query_part, NT)
            dp_ref[...] = dot(value_part, do_part, NT)
            lse = lse_ref[head : head + 1, rows]
            outdot = outdot_ref[head : head + 1, rows]

            def step(index, carry):
                at = pl.ds(pl.multiple_of(index * PIECE, PIECE), PIECE)
                tile = s_ref[at, :] + block_bias(bias_ref, places, head, index, q_chunk * blocks, blocks)
                ok = places[8 + index] * PIECE + key_iota < length
                prob = jnp.exp(jnp.where(ok, tile, NEG_FILL) - lse)
                p_ref[at, :] = prob.astype(BF16)
                grad = prob * (dp_ref[at, :] - outdot)
                ds_ref[at, :] = grad.astype(BF16)
                for i in range(blocks):
                    apart = places[8 + index] - places[q_chunk * blocks + i]
                    which = jnp.clip(apart, -2, 2) + 2
                    tile_ref[head, which] += grad[:, i * PIECE : (i + 1) * PIECE]
                return carry

            repeat(key_blocks, unroll, step, 0)
            dk = dot(ds_ref[...], query_part)
            dv = dot(p_ref[...], do_part)
            k_lanes, v_lanes = lanes, slice(COLS + head * DH, COLS + head * DH + DH)
            dkv_sum[:, k_lanes] += dk
            dkv_sum[:, v_lanes] += dv
            dqt_ref[lanes, rows] = dot(key_part, ds_ref[...], TN)
            return carry

        repeat(GROUP // chunk, unroll, for_queries, 0)
    dq_ref[...] = dqt_ref[...].T.astype(BF16)
    dkv_ref[...] = dkv_sum[...].astype(BF16)
    table_ref[...] = jnp.zeros_like(table_ref)
    apart = lax.broadcasted_iota(jnp.int32, (PIECE, PIECE), 0) - lax.broadcasted_iota(
        jnp.int32, (PIECE, PIECE), 1
    )
    for head in range(HEADS):
        for which in range(5):
            tile = tile_ref[head, which]
            if which in (0, 4):
                b = 15 if which == 0 else 31
                table_ref[head, b : b + 1, :] += jnp.sum(tile, axis=0, keepdims=True)
                continue
            ids = bucket_index(apart + (which - 2) * PIECE)
            low, high = ((1, 16), (0, 32), (17, 32))[which - 1]
            for b in range(low, high):
                part = jnp.sum(jnp.where(ids == b, tile, 0.0), axis=0, keepdims=True)
                table_ref[head, b : b + 1, :] += part


def vmem():
    return pl.BlockSpec(memory_space=pltpu.VMEM)


def smem():
    return pl.BlockSpec(memory_space=pltpu.SMEM)


def shape(dims, dtype):
    return jax.ShapeDtypeStruct(dims, dtype)


PARAMS = pltpu.CompilerParams(vmem_limit_bytes=56 * 1024 * 1024)


def attention(places, q, kv, offsets, bias, out_w, chunk):
    keys = kv.shape[0]
    return pl.pallas_call(
        functools.partial(attention_kernel, chunk, offsets),
        out_shape=(
            shape((GROUP // 2, D), F32),
            shape((GROUP // 2, D), BF16),
            shape((COLS, GROUP), F32),
            shape((8, GROUP), F32),
        ),
        in_specs=[smem()] + [vmem()] * 4,
        out_specs=(vmem(),) * 4,
        scratch_shapes=[pltpu.VMEM((keys, chunk), F32), pltpu.VMEM((keys, chunk), BF16)],
        compiler_params=PARAMS,
        cost_estimate=pl.CostEstimate(
            flops=4 * GROUP * keys * COLS, bytes_accessed=8 * 2**20, transcendentals=GROUP * keys * HEADS
        ),
    )(places, q, kv, bias, out_w)


def attention_back(places, q, kv, offsets, bias, out_w, up, attn_t, lse, chunk):
    keys = kv.shape[0]
    return pl.pallas_call(
        functools.partial(attention_back_kernel, chunk, offsets),
        out_shape=(
            shape((GROUP, COLS), BF16),
            shape((keys, 2 * COLS), BF16),
            shape((HEADS, BUCKETS, PIECE), F32),
        ),
        in_specs=[smem()] + [vmem()] * 7,
        out_specs=(vmem(),) * 3,
        scratch_shapes=[
            pltpu.VMEM((keys, chunk), F32),
            pltpu.VMEM((keys, chunk), F32),
            pltpu.VMEM((keys, chunk), BF16),
            pltpu.VMEM((keys, chunk), BF16),
            pltpu.VMEM((GROUP, COLS), BF16),
            pltpu.VMEM((8, GROUP), F32),
            pltpu.VMEM((COLS, GROUP), F32),
            pltpu.VMEM((keys, 2 * COLS), F32),
            pltpu.VMEM((HEADS, 5, PIECE, PIECE), F32),
        ],
        compiler_params=PARAMS,
        cost_estimate=pl.CostEstimate(
            flops=10 * GROUP * keys * COLS, bytes_accessed=12 * 2**20, transcendentals=GROUP * keys * HEADS
        ),
    )(places, q, kv, bias, out_w, up, attn_t, lse)


def on_device(
    inputs, teacher, seq_lengths, gain_attn, w_query, w_key, w_value, w_out, bias_table, gain_ffn, w_inner, w_outer
):
    n_ctx = lax.axis_size("ctx")
    spread = n_ctx // (SEQ_DEV * TP)
    me = lax.axis_index("wsh")
    ctx_me = lax.axis_index("ctx")
    parity = ctx_me & 1
    token_total = ROWS * n_ctx * TP
    same, cross = seq_routes(n_ctx)
    home = ctx_me // spread
    stretch = ctx_me % spread
    seq_bit = home & 1

    def to_home(pair):
        near = lax.ppermute(pick(pair, parity), AXES, same)
        far = lax.ppermute(pick(pair, 1 - parity), AXES, cross)
        return near, far

    def from_home(rows):
        near = lax.ppermute(rows[:PIECE], AXES, backwards(same))
        far = lax.ppermute(rows[PIECE:], AXES, backwards(cross))
        return jnp.where(parity == 0, jnp.stack([near, far]), jnp.stack([far, near]))

    def block_places(stretch_index):
        return [
            TP * 2 * stretch_index + 2 * swapped(me ^ r) + (seq_bit ^ e) for r in ORDER for e in (0, 1)
        ]

    query_blocks = block_places(stretch)
    key_blocks = [p for i in range(spread) for p in block_places(i)] if spread > 1 else query_blocks
    length = lax.ppermute(pick(seq_lengths, parity), AXES, same)
    places = jnp.stack(query_blocks + key_blocks + [length])

    near, far = to_home(inputs)
    x_low = jnp.concatenate([near, far])
    teacher_rows = jnp.concatenate(to_home(teacher))

    counts = jnp.sum(jnp.minimum(seq_lengths, n_ctx * PIECE)).astype(F32).reshape(1, 1)
    counts = counts + to_partner(counts, 1)
    valid_count = (counts + to_partner(counts, 2))[0, 0]

    small = jnp.concatenate([gain_attn, gain_ffn, bias_table.reshape(-1)])
    small_all = by_owner([small] + [to_partner(small, r) for r in (1, 2, 3)], me)
    attn_gain = small_all[:, :192].reshape(1, D).astype(F32)
    ffn_gain = small_all[:, 192:384].reshape(1, D).astype(F32)
    table = small_all[:, 384:].reshape(BUCKETS, TP, HEADS)
    my_table = lax.dynamic_index_in_dim(table, me, 1, keepdims=False).T.astype(F32)

    qkv_blocks = (
        jnp.stack([w_query, w_key, w_value], axis=1).reshape(192, 3, TP, COLS).transpose(2, 0, 1, 3)
    ).reshape(TP, 192, 3 * COLS)
    w_qkv = exchange_blocks(qkv_blocks, me).reshape(D, 3 * COLS)
    inner_blocks = w_inner.reshape(192, TP, D).transpose(1, 0, 2)
    w_in = exchange_blocks(inner_blocks, me).reshape(D, D)

    shift = (jnp.arange(5, dtype=jnp.int32) - 2)[:, None, None] * PIECE
    spot = jnp.arange(PIECE, dtype=jnp.int32)
    buckets = bucket_index(shift + spot[None, :, None] - spot[None, None, :])
    bias = jnp.zeros((HEADS,) + buckets.shape, F32)
    for b in range(BUCKETS):
        bias = jnp.where(buckets[None] == b, my_table[:, b, None, None, None], bias)

    x_all = gather_group(x_low).astype(F32)
    normed = (x_all * lax.rsqrt(jnp.mean(x_all * x_all, axis=-1, keepdims=True) + EPS) * attn_gain).astype(BF16)
    qkv = dot(normed, w_qkv).astype(BF16)
    if spread == 1:
        q, kv, offsets = qkv, qkv, (COLS, 2 * COLS)
        chunk = 256
    else:
        teams = [[s * spread + i for i in range(spread)] for s in range(SEQ_DEV * TP)]
        q, offsets = qkv[:, :COLS], (0, COLS)
        kv = lax.all_gather(qkv[:, COLS:], "ctx", axis=0, tiled=True, axis_index_groups=teams)
        chunk = 128
    keep, send, attn_t, lse = attention(places, q, kv, offsets, bias, w_out, chunk)
    x_rows = x_low.astype(F32)
    hidden = x_rows + scatter_group(keep, send)
    ffn_scale = lax.rsqrt(jnp.mean(hidden * hidden, axis=-1, keepdims=True) + EPS)
    ffn_low = (hidden * ffn_scale * ffn_gain).astype(BF16)
    ffn_all = gather_group(ffn_low)
    inner = dot(ffn_all, w_in)
    active, slope = gelu_and_slope(inner)
    active_low = active.astype(BF16)
    partial = dot(active_low, w_outer)
    result = hidden + scatter_group(partial[: GROUP // 2], partial[GROUP // 2 :].astype(BF16))

    layer_out = from_home(result.astype(BF16))
    row_places = jnp.concatenate([query_blocks[e] * PIECE + spot for e in (0, 1)])
    row_valid = (row_places < length).astype(F32)[:, None]
    deviation = result - teacher_rows.astype(F32)
    square_sum = jnp.sum(deviation * deviation * row_valid)
    result_grad = token_total / valid_count * deviation * row_valid

    result_all = gather_group(result_grad.astype(BF16))
    active_grad = dot(result_all, w_outer, NT)
    inner_grad = (slope * active_grad).astype(BF16)
    partial = dot(inner_grad, w_in, NT)
    outer_wgrad = dot(active_low, result_all, TN)
    inner_wgrad = dot(ffn_all, inner_grad, TN)
    ffn_grad = scatter_group(partial[: GROUP // 2], partial[GROUP // 2 :].astype(BF16))
    unit = hidden * ffn_scale
    ffn_gain_grad = jnp.sum(ffn_grad * unit, axis=0)
    scaled = ffn_gain * ffn_grad
    hidden_grad = result_grad + ffn_scale * (scaled - unit * jnp.mean(scaled * unit, axis=-1, keepdims=True))
    hidden_all = gather_group(hidden_grad.astype(BF16))
    dq, dkv, table_part = attention_back(
        places, q, kv, offsets, bias, w_out, hidden_all, attn_t, lse, chunk
    )
    if spread > 1:
        dkv = lax.psum_scatter(dkv, "ctx", scatter_dimension=0, tiled=True, axis_index_groups=teams)
    d_qkv = jnp.concatenate([dq, dkv], axis=1)
    partial = dot(d_qkv, w_qkv, NT)
    out_wgrad = dot(attn_t.astype(BF16), hidden_all)
    qkv_wgrad = dot(normed, d_qkv, TN)
    normed_grad = scatter_group(partial[: GROUP // 2], partial[GROUP // 2 :].astype(BF16))
    scale = lax.rsqrt(jnp.mean(x_rows * x_rows, axis=-1, keepdims=True) + EPS)
    unit = x_rows * scale
    attn_gain_grad = jnp.sum(normed_grad * unit, axis=0)
    scaled = attn_gain * normed_grad
    input_grad = hidden_grad + scale * (scaled - unit * jnp.mean(scaled * unit, axis=-1, keepdims=True))
    input_grad = from_home(input_grad.astype(BF16)).astype(F32)

    def natural(grad):
        parts = grad.reshape((n_ctx, grad.shape[0] // n_ctx) + grad.shape[1:])
        return gather_ctx(reduce_ctx(parts, ctx_me), ctx_me).reshape(grad.shape).astype(F32)

    def columns(grad):
        cols = grad.shape[1]
        depth = 192 // n_ctx
        parts = grad.reshape(TP, n_ctx, depth, cols).transpose(1, 0, 2, 3)
        chunk_sum = reduce_ctx(parts, ctx_me).astype(BF16)
        mine = exchange_blocks(chunk_sum, me)
        rows = gather_ctx(mine.transpose(1, 0, 2), ctx_me)
        return rows.reshape(192, TP, cols).astype(F32)

    w_outer_grad = natural(outer_wgrad)
    w_inner_grad = columns(inner_wgrad).reshape(192, TP * D)
    w_out_grad = natural(out_wgrad)
    qkv_rows = columns(qkv_wgrad).reshape(192, TP, 3, COLS)
    w_query_grad, w_key_grad, w_value_grad = (qkv_rows[:, :, i].reshape(192, D) for i in range(3))

    table_part = jnp.sum(table_part, axis=-1)
    table_spread = lax.dynamic_update_slice(
        jnp.zeros((BUCKETS, TP, HEADS), F32), table_part.T[:, None, :], (0, me, 0)
    )
    totals = lax.psum(
        jnp.concatenate([attn_gain_grad, ffn_gain_grad, table_spread.reshape(-1), square_sum.reshape(1)]), AXES
    )
    my_attn_gain = lax.dynamic_slice(totals, (me * 192,), (192,))
    my_ffn_gain = lax.dynamic_slice(totals, (D + me * 192,), (192,))
    my_rows = lax.dynamic_slice(totals, (2 * D + me * 8 * H,), (8 * H,)).reshape(8, H)
    loss_value = totals[2 * D + BUCKETS * H] / (valid_count * D)
    return (
        layer_out,
        loss_value,
        input_grad,
        my_attn_gain,
        w_query_grad,
        w_key_grad,
        w_value_grad,
        w_out_grad,
        my_rows,
        my_ffn_gain,
        w_inner_grad,
        w_outer_grad,
    )


def solution(mesh):
    rows = P("wsh", None)
    tokens = P("wsh", "ctx", None)
    return jax.shard_map(
        on_device,
        mesh=mesh,
        in_specs=(tokens, tokens, P("wsh"), P("wsh"), rows, rows, rows, rows, rows, P("wsh"), rows, rows),
        out_specs=(tokens, P(), tokens, P("wsh"), rows, rows, rows, rows, rows, P("wsh"), rows, rows),
        check_vma=False,
    )
```

time: 1090 us -> 446 us (0.41)
  waiting for transfers between devices: 555 us -> 143 us
  blocking collectives: 340 us -> 43.9 us
  starting transfers between devices: 3.31 us -> 93.7 us
  matrix products: 97.1 us -> 25.9 us
  Pallas kernels: 0 us -> 28.5 us
  local copies, waits for them, and re-layouts: 35.9 us -> 61.8 us
  between operations: 20.9 us -> 6.24 us
    psum x2 -> x1, blocking collectives: 319 us -> 43.9 us  [on_device(): lax.psum(jnp.concatenate([attn_gain_grad, ffn_gain_grad, table_spread.res...]
    ppermute x22 -> x78, waiting for transfers between devices: 374 us -> 143 us  [the longest x32 82.6 us: to_ctx(): return lax.ppermute(value, 'ctx', [(i, i ^ offset) for i in range(n_ctx)])]
    reduce_scatter x6 -> x0, waiting for transfers between devices: 149 us -> none  [the longest x1 50.5 us: on_device(): lax.psum_scatter(local_grads[8].astype(jnp.bfloat16), 'wsh', scatter_dime...]
    ppermute x22 -> x78, starting transfers between devices: 2.84 us -> 93.7 us  [the longest x32 42.8 us: to_ctx(): return lax.ppermute(value, 'ctx', [(i, i ^ offset) for i in range(n_ctx)])]
    dot_general x96 -> x10, matrix products: 97.1 us -> 25.9 us  [dot(): return lax.dot_general(left, right, dims, preferred_element_type=F32)]
    pallas_call x0 -> x2, Pallas kernels: none -> 28.5 us  [the longest x1 15.3 us: attention_back(): pl.pallas_call(functools.partial(attention_back_kernel, chunk, offsets),...]
    all_gather x6 -> x0, waiting for transfers between devices: 28 us -> none  [the longest x1 14.1 us: on_device(): lax.all_gather(shards[3], 'wsh', axis=0, tiled=True)]
    while x162 -> x0, local copies, waits for them, and re-layouts: 19.1 us -> none
  transfers between devices with their start and end apart: 34 -> 78, of which waited for: 28 -> 32; matrix products, arithmetic and copies ran while one was open for 12% -> 21% of each run, Pallas kernels for 0% -> 4%
where the time goes in v1:
time: 446 us; the launch traced here: 438 us
  waiting for transfers between devices  143 us (32%)
  starting transfers between devices  93.7 us (21%)
  local copies, waits for them, and re-layouts  61.8 us (14%)
  blocking collectives  43.9 us (10%)
  other arithmetic  34.6 us (8%)
  Pallas kernels  28.5 us (6%)
  matrix products  25.9 us (6%)
  between operations  6.24 us (1%)
    ppermute x32, waiting for transfers between devices, to_ctx(): return lax.ppermute(value, 'ctx', [(i, i ^ offset) for i in range(n_ctx)])  82.6 us
    ppermute x37, waiting for transfers between devices, to_partner(): return lax.ppermute(value, 'wsh', [(i, i ^ offset) for i in range(TP)])  48.4 us
    psum x1, blocking collectives, on_device(): lax.psum(jnp.concatenate([attn_gain_grad, ffn_gain_grad, table_spread.res...  43.9 us
    ppermute x32, starting transfers between devices, to_ctx(): return lax.ppermute(value, 'ctx', [(i, i ^ offset) for i in range(n_ctx)])  42.8 us
    dot_general x10, matrix products, dot(): return lax.dot_general(left, right, dims, preferred_element_type=F32)  25.9 us
    ppermute x37, starting transfers between devices, to_partner(): return lax.ppermute(value, 'wsh', [(i, i ^ offset) for i in range(TP)])  24.6 us
    pallas_call x1, Pallas kernels, attention_back(): pl.pallas_call(functools.partial(attention_back_kernel, chunk, offsets),...  15.3 us
    pallas_call x1, Pallas kernels, attention(): pl.pallas_call(functools.partial(attention_kernel, chunk, offsets), out_s...  13.2 us
  transfers between devices with their start and end apart: 78, of which 32 were waited for; matrix products, arithmetic and copies ran while one was open for 21% of the time, Pallas kernels for 4%

profile of v1, /device:TPU:4, one launch (start us, length us, event | category | flops | bytes accessed | tf_op | source)
XLA Modules:
  0.0 437.6 jit_solution(13670036583100760602)
XLA Ops:
  31.9 5.2 %select_select_fusion.bias_ref = f32[3,5,128,128]{3,2,1,0:T(8,128)} fusion(f32[3]{0:T(128)S(1)} %get-tuple-element.31, f32[3]{0:T(128)S(1)} %get-tuple-element.32, f32[3]{0:T(128)S(1)} %get-tuple-element.33, f32[3]{0:T(128)S(1)} %get-tuple-element.34, f32[3]{0:T(128)S(1)} %get-tuple-element.35, f32[3]{0:T(128)S(1)} %get-tuple-element.36, ...), kind=kLoop, calls=%fused_computation.58 | loop fusion | flops 7864320 | bytes 3604864 | tf_op jit(solution)/shard_map/jit(_where)/select_n | solution.py:401
  37.1 3.9 collective-permute-done
  47.4 6.2 %collective-permute-done.3 = bf16[256,768]{1,0:T(8,128)(2,1)} collective-permute-done((bf16[256,768]{1,0:T(8,128)(2,1)S(1)}, bf16[256,768]{1,0:T(8,128)(2,1)}, u32[]{:S(2)}, u32[]{:S(2)}) %collective-permute-start.3) | collective-permute-done | bytes 393248 | tf_op jit(solution)/shard_map/ppermute | solution.py:60
  62.8 4.0 convolution_convert_fusion.q_ref.kv_ref
  66.8 13.2 %shard_map.211 = (f32[512,768]{1,0:T(8,128)}, bf16[512,768]{1,0:T(8,128)(2,1)}, f32[192,1024]{1,0:T(8,128)}, f32[8,1024]{1,0:T(8,128)}) custom-call(s32[17]{0:T(128)} %stack.333.places, bf16[1024,576]{1,0:T(8,128)(2,1)} %convolution_convert_fusion.q_ref.kv_ref, bf16[1024,576]{1,0:T(8,128)(2,1)} %convolution_convert_fusion.q_ref.kv_ref, ...), custom_call_target="tpu_custom_call" | custom-call | flops 805306368 | bytes 8388608 | tf_op jit(solution)/shard_map/pallas_call | solution.py:293
  89.8 8.2 %collective-permute-done.13 = bf16[256,768]{1,0:T(8,128)(2,1)} collective-permute-done((bf16[256,768]{1,0:T(8,128)(2,1)S(1)}, bf16[256,768]{1,0:T(8,128)(2,1)}, u32[]{:S(2)}, u32[]{:S(2)}) %collective-permute-start.13) | collective-permute-done | bytes 393248 | tf_op jit(solution)/shard_map/ppermute | solution.py:60
  105.8 6.6 %collective-permute-done.14 = bf16[256,768]{1,0:T(8,128)(2,1)S(1)} collective-permute-done((bf16[256,768]{1,0:T(8,128)(2,1)S(1)}, bf16[256,768]{1,0:T(8,128)(2,1)S(1)}, u32[]{:S(2)}, u32[]{:S(2)}) %collective-permute-start.14) | collective-permute-done | bytes 393248 | tf_op jit(solution)/shard_map/ppermute | solution.py:60
  112.4 4.1 collective-permute-done.19
  116.5 7.0 %collective-permute-done.18 = bf16[192,768]{1,0:T(8,128)(2,1)S(1)} collective-permute-done((bf16[192,768]{1,0:T(8,128)(2,1)S(1)}, bf16[192,768]{1,0:T(8,128)(2,1)S(1)}, u32[]{:S(2)}, u32[]{:S(2)}) %collective-permute-start.18) | collective-permute-done | bytes 294944 | tf_op jit(solution)/shard_map/ppermute | solution.py:60
  124.0 4.9 %multiply_convert_fusion = (bf16[1024,768]{1,0:T(8,128)(2,1)S(1)}, f32[1024,768]{1,0:T(8,128)}) fusion(bf16[768,768]{1,0:T(8,128)(2,1)S(1)} %bitcast.252, bf16[256,768]{1,0:T(8,128)(2,1)S(1)} %collective-permute-done.16, bf16[256,768]{1,0:T(8,128)(2,1)S(1)} %collective-permute-done.15, bf16[256,768]{1,0:T(8,128)(2,1)S(1)} %collective-permute-done.14, ...), kind=kOutput, calls=%fused_computation.12 | convolution fusion | flops 1218183168 | bytes 7471104 | tf_op jit(solution)/shard_map/dot_general | solution.py:35
  138.7 4.1 collective-permute-start.26
  148.9 6.1 %collective-permute-done.27 = bf16[128,768]{1,0:T(8,128)(2,1)} collective-permute-done((bf16[128,768]{1,0:T(8,128)(2,1)}, bf16[128,768]{1,0:T(8,128)(2,1)}, u32[]{:S(2)}, u32[]{:S(2)}) %collective-permute-start.27) | collective-permute-done | bytes 196640 | tf_op jit(solution)/shard_map/ppermute | solution.py:356
  158.8 8.0 %collective-permute-done.28 = bf16[256,768]{1,0:T(8,128)(2,1)S(1)} collective-permute-done((bf16[256,768]{1,0:T(8,128)(2,1)}, bf16[256,768]{1,0:T(8,128)(2,1)S(1)}, u32[]{:S(2)}, u32[]{:S(2)}) %collective-permute-start.28) | collective-permute-done | bytes 393248 | tf_op jit(solution)/shard_map/ppermute | solution.py:60
  171.1 4.9 %fusion.8 = bf16[1024,768]{1,0:T(8,128)(2,1)S(1)} fusion(f32[1024,768]{1,0:T(8,128)} %get-tuple-element.207, bf16[768,768]{1,0:T(8,128)(2,1)S(1)} %copy-done, bf16[256,768]{1,0:T(8,128)(2,1)} %copy-done.35, bf16[256,768]{1,0:T(8,128)(2,1)} %copy-done.33, bf16[256,768]{1,0:T(8,128)(2,1)S(1)} %collective-permute-done.28, bf16[256,768]{1,0:T(8,128)(2,1)} %get-tuple-element.64), kind=kOutput, calls=%fused_computation.11 | convolution fusion | flops 1222115328 | bytes 7471104 | tf_op jit(solution)/shard_map/dot_general | solution.py:35
  185.0 9.2 %collective-permute-done.59 = bf16[4,4,24,768]{3,2,1,0:T(8,128)(2,1)S(1)} collective-permute-done((bf16[4,4,24,768]{3,2,1,0:T(8,128)(2,1)S(1)}, bf16[4,4,24,768]{3,2,1,0:T(8,128)(2,1)S(1)}, u32[]{:S(2)}, u32[]{:S(2)}) %collective-permute-start.59) | collective-permute-done | bytes 589856 | tf_op jit(solution)/shard_map/ppermute | solution.py:65
  196.2 10.5 %collective-permute-done.70 = bf16[4,96,768]{2,1,0:T(8,128)(2,1)S(1)} collective-permute-done((bf16[4,96,768]{2,1,0:T(8,128)(2,1)S(1)}, bf16[4,96,768]{2,1,0:T(8,128)(2,1)S(1)}, u32[]{:S(2)}, u32[]{:S(2)}) %collective-permute-start.70) | collective-permute-done | bytes 589856 | tf_op jit(solution)/shard_map/ppermute | solution.py:65
  210.4 5.7 %collective-permute-done.60 = bf16[4,24,768]{2,1,0:T(8,128)(2,1)S(1)} collective-permute-done((bf16[4,24,768]{2,1,0:T(8,128)(2,1)S(1)}, bf16[4,24,768]{2,1,0:T(8,128)(2,1)S(1)}, u32[]{:S(2)}, u32[]{:S(2)}) %collective-permute-start.60) | collective-permute-done | bytes 147488 | tf_op jit(solution)/shard_map/ppermute | solution.py:65
  217.3 6.1 %collective-permute-done.72 = bf16[96,768]{1,0:T(8,128)(2,1)S(1)} collective-permute-done((bf16[96,768]{1,0:T(8,128)(2,1)S(1)}, bf16[96,768]{1,0:T(8,128)(2,1)S(1)}, u32[]{:S(2)}, u32[]{:S(2)}) %collective-permute-start.72) | collective-permute-done | bytes 147488 | tf_op jit(solution)/shard_map/ppermute | solution.py:65
  233.0 4.7 %collective-permute-start.67 = (bf16[24,4,768]{2,0,1:T(8,128)(2,1)S(1)}, bf16[24,4,768]{2,0,1:T(8,128)(2,1)S(1)}, u32[]{:S(2)}, u32[]{:S(2)}) collective-permute-start(bf16[24,4,768]{2,0,1:T(8,128)(2,1)S(1)} %get-tuple-element.141), channel_id=1, source_target_pairs={{0,16},{4,20},{8,24},{12,28},{16,0},{20,4},{24,8},{28,12},{1,17},{... | collective-permute-start | bytes 442376 | tf_op jit(solution)/shard_map/ppermute | solution.py:65
  237.6 8.0 %collective-permute-done.75 = bf16[96,768]{1,0:T(8,128)(2,1)S(1)} collective-permute-done((bf16[96,768]{1,0:T(8,128)(2,1)S(1)}, bf16[96,768]{1,0:T(8,128)(2,1)S(1)}, u32[]{:S(2)}, u32[]{:S(2)}) %collective-permute-start.75) | collective-permute-done | bytes 147488 | tf_op jit(solution)/shard_map/ppermute | solution.py:65
  248.1 5.0 %collective-permute-start.22 = (bf16[128,768]{1,0:T(8,128)(2,1)S(1)}, bf16[128,768]{1,0:T(8,128)(2,1)S(1)}, u32[]{:S(2)}, u32[]{:S(2)}) collective-permute-start(bf16[128,768]{1,0:T(8,128)(2,1)S(1)} %get-tuple-element.127), channel_id=1, source_target_pairs={{0,0},{16,1},{8,2},{24,3},{4,4},{20,5},{12,6},{28,7},{2,8},{18,9},... | collective-permute-start | bytes 589832 | tf_op jit(solution)/shard_map/ppermute | solution.py:360
  257.9 4.7 %collective-permute-start.33 = (bf16[256,768]{1,0:T(8,128)(2,1)S(1)}, bf16[256,768]{1,0:T(8,128)(2,1)S(1)}, u32[]{:S(2)}, u32[]{:S(2)}) collective-permute-start(bf16[256,768]{1,0:T(8,128)(2,1)S(1)} %get-tuple-element.62), channel_id=1, source_target_pairs={{0,2},{1,3},{2,0},{3,1},{4,6},{5,7},{6,4},{7,5},{8,10},{9,11},{10,... | collective-permute-start | bytes 1179656 | tf_op jit(solution)/shard_map/ppermute | solution.py:60
  263.5 6.0 %collective-permute-done.77 = bf16[4,96,768]{2,1,0:T(8,128)(2,1)S(1)} collective-permute-done((bf16[4,96,768]{2,1,0:T(8,128)(2,1)S(1)}, bf16[4,96,768]{2,1,0:T(8,128)(2,1)S(1)}, u32[]{:S(2)}, u32[]{:S(2)}) %collective-permute-start.77) | collective-permute-done | bytes 589856 | tf_op jit(solution)/shard_map/ppermute | solution.py:65
  271.7 8.2 %collective-permute-done.69 = bf16[4,24,4,768]{3,1,2,0:T(8,128)(2,1)S(1)} collective-permute-done((bf16[4,24,4,768]{3,1,2,0:T(8,128)(2,1)S(1)}, bf16[4,24,4,768]{3,1,2,0:T(8,128)(2,1)S(1)}, u32[]{:S(2)}, u32[]{:S(2)}) %collective-permute-start.69) | collective-permute-done | bytes 589856 | tf_op jit(solution)/shard_map/ppermute | solution.py:65
  285.6 15.3 %shard_map.212 = (bf16[1024,192]{1,0:T(8,128)(2,1)}, bf16[1024,384]{1,0:T(8,128)(2,1)}, f32[3,32,128]{2,1,0:T(8,128)}) custom-call(s32[17]{0:T(128)} %stack.333.places, bf16[1024,576]{1,0:T(8,128)(2,1)} %convolution_convert_fusion.q_ref.kv_ref, bf16[1024,576]{1,0:T(8,128)(2,1)} %convolution_convert_fusion.q_ref.kv_ref, ...), custom_call_target="tpu_custom_call" | custom-call | flops 2013265920 | bytes 12582912 | tf_op jit(solution)/shard_map/pallas_call | solution.py:313
  326.6 3.7 collective-permute-done.43
  330.2 4.4 collective-permute-done.42
  343.6 3.6 collective-permute-done.49
  347.2 4.9 %collective-permute-done.48 = bf16[24,4,576]{2,0,1:T(8,128)(2,1)S(1)} collective-permute-done((bf16[24,4,576]{2,0,1:T(8,128)(2,1)S(1)}, bf16[24,4,576]{2,0,1:T(8,128)(2,1)S(1)}, u32[]{:S(2)}, u32[]{:S(2)}) %collective-permute-start.48) | collective-permute-done | bytes 110624 | tf_op jit(solution)/shard_map/ppermute | solution.py:65
  356.1 9.5 %collective-permute-done.50 = bf16[4,24,4,576]{3,1,2,0:T(8,128)(2,1)S(1)} collective-permute-done((bf16[4,24,4,576]{3,1,2,0:T(8,128)(2,1)S(1)}, bf16[4,24,4,576]{3,1,2,0:T(8,128)(2,1)S(1)}, u32[]{:S(2)}, u32[]{:S(2)}) %collective-permute-start.50) | collective-permute-done | bytes 442400 | tf_op jit(solution)/shard_map/ppermute | solution.py:65
  382.5 5.4 %collective-permute-start.38 = (bf16[128,768]{1,0:T(8,128)(2,1)S(1)}, bf16[128,768]{1,0:T(8,128)(2,1)S(1)}, u32[]{:S(2)}, u32[]{:S(2)}) collective-permute-start(bf16[128,768]{1,0:T(8,128)(2,1)S(1)} %get-tuple-element.122), channel_id=1, source_target_pairs={{0,0},{16,1},{8,2},{24,3},{4,4},{20,5},{12,6},{28,7},{2,8},{18,9},... | collective-permute-start | bytes 589832 | tf_op jit(solution)/shard_map/ppermute | solution.py:360
  388.6 43.9 %psum.7 = f32[1921]{0:T(1024)S(1)} all-reduce(f32[1921]{0:T(1024)S(1)} %pad_maximum_fusion.29), channel_id=1, replica_groups=mesh['ctx'=8,'wsh'=4] {'ctx','wsh'}, use_global_device_ids=true, to_apply=%region_9.10 | all-reduce | flops 1921 | bytes 15368 | tf_op jit(solution)/shard_map/psum | solution.py:485
  (373 shorter events, 186.4 us)
Async XLA Ops:
  2.9 20.0 %collective-permute-start.8 = (bf16[480]{0:T(512)(128)(2,1)}, bf16[480]{0:T(512)(128)(2,1)}, u32[]{:S(2)}, u32[]{:S(2)}) collective-permute-start(bf16[480]{0:T(512)(128)(2,1)} %pad_maximum_fusion.33), channel_id=1, source_target_pairs={{0,3},{1,2},{2,1},{3,0},{4,7},{5,6},{6,5},{7,4},{8,11},{9,10},{10,... | collective-permute-start | bytes 2888 | tf_op jit(solution)/shard_map/ppermute | solution.py:60
  2.9 20.7 %collective-permute-start.7 = (bf16[480]{0:T(512)(128)(2,1)}, bf16[480]{0:T(512)(128)(2,1)}, u32[]{:S(2)}, u32[]{:S(2)}) collective-permute-start(bf16[480]{0:T(512)(128)(2,1)} %pad_maximum_fusion.33), channel_id=1, source_target_pairs={{0,2},{1,3},{2,0},{3,1},{4,6},{5,7},{6,4},{7,5},{8,10},{9,11},{10,... | collective-permute-start | bytes 2888 | tf_op jit(solution)/shard_map/ppermute | solution.py:60
  4.3 22.3 %collective-permute-start.6 = (bf16[480]{0:T(512)(128)(2,1)}, bf16[480]{0:T(512)(128)(2,1)}, u32[]{:S(2)}, u32[]{:S(2)}) collective-permute-start(bf16[480]{0:T(512)(128)(2,1)} %pad_maximum_fusion.33), channel_id=1, source_target_pairs={{0,1},{1,0},{2,3},{3,2},{4,5},{5,4},{6,7},{7,6},{8,9},{9,8},{10,11... | collective-permute-start | bytes 2888 | tf_op jit(solution)/shard_map/ppermute | solution.py:60
  13.1 32.2 %collective-permute-start.11 = (bf16[192,576]{0,1:T(8,128)(2,1)}, bf16[192,576]{0,1:T(8,128)(2,1)}, u32[]{:S(2)}, u32[]{:S(2)}) collective-permute-start(bf16[192,576]{0,1:T(8,128)(2,1)} %get-tuple-element.95), channel_id=1, source_target_pairs={{0,3},{1,2},{2,1},{3,0},{4,7},{5,6},{6,5},{7,4},{8,11},{9,10},{10,... | collective-permute-start | bytes 663560 | tf_op jit(solution)/shard_map/ppermute | solution.py:60
  19.1 26.1 %collective-permute-start.10 = (bf16[192,576]{0,1:T(8,128)(2,1)}, bf16[192,576]{0,1:T(8,128)(2,1)S(1)}, u32[]{:S(2)}, u32[]{:S(2)}) collective-permute-start(bf16[192,576]{0,1:T(8,128)(2,1)} %get-tuple-element.96), channel_id=1, source_target_pairs={{0,2},{1,3},{2,0},{3,1},{4,6},{5,7},{6,4},{7,5},{8,10},{9,11},{10,... | collective-permute-start | bytes 663560 | tf_op jit(solution)/shard_map/ppermute | solution.py:60
  22.9 22.4 %collective-permute-start.9 = (bf16[192,576]{0,1:T(8,128)(2,1)}, bf16[192,576]{0,1:T(8,128)(2,1)}, u32[]{:S(2)}, u32[]{:S(2)}) collective-permute-start(bf16[192,576]{0,1:T(8,128)(2,1)} %get-tuple-element.97), channel_id=1, source_target_pairs={{0,1},{1,0},{2,3},{3,2},{4,5},{5,4},{6,7},{7,6},{8,9},{9,8},{10,11... | collective-permute-start | bytes 663560 | tf_op jit(solution)/shard_map/ppermute | solution.py:60
  23.5 17.5 %collective-permute-start = (bf16[128,768]{1,0:T(8,128)(2,1)}, bf16[128,768]{1,0:T(8,128)(2,1)}, u32[]{:S(2)}, u32[]{:S(2)}) collective-permute-start(bf16[128,768]{1,0:T(8,128)(2,1)} %get-tuple-element.130), channel_id=1, source_target_pairs={{0,0},{1,16},{2,8},{3,24},{4,4},{5,20},{6,12},{7,28},{8,2},{9,18},... | collective-permute-start | bytes 589832 | tf_op jit(solution)/shard_map/ppermute | solution.py:355
  26.6 16.8 %collective-permute-start.1 = (bf16[128,768]{1,0:T(8,128)(2,1)}, bf16[128,768]{1,0:T(8,128)(2,1)}, u32[]{:S(2)}, u32[]{:S(2)}) collective-permute-start(bf16[128,768]{1,0:T(8,128)(2,1)} %get-tuple-element.129), channel_id=1, source_target_pairs={{0,4},{1,20},{2,12},{3,28},{4,0},{5,16},{6,8},{7,24},{8,6},{9,22},... | collective-permute-start | bytes 589832 | tf_op jit(solution)/shard_map/ppermute | solution.py:356
  103.8 19.7 %collective-permute-start.18 = (bf16[192,768]{1,0:T(8,128)(2,1)S(1)}, bf16[192,768]{1,0:T(8,128)(2,1)S(1)}, u32[]{:S(2)}, u32[]{:S(2)}) collective-permute-start(bf16[192,768]{1,0:T(8,128)(2,1)S(1)} %bitcast.270), channel_id=1, source_target_pairs={{0,2},{1,3},{2,0},{3,1},{4,6},{5,7},{6,4},{7,5},{8,10},{9,11},{10,... | collective-permute-start | bytes 884744 | tf_op jit(solution)/shard_map/ppermute | solution.py:60
  105.1 18.5 %collective-permute-start.17 = (bf16[192,768]{1,0:T(8,128)(2,1)S(1)}, bf16[192,768]{1,0:T(8,128)(2,1)S(1)}, u32[]{:S(2)}, u32[]{:S(2)}) collective-permute-start(bf16[192,768]{1,0:T(8,128)(2,1)S(1)} %bitcast.271), channel_id=1, source_target_pairs={{0,1},{1,0},{2,3},{3,2},{4,5},{5,4},{6,7},{7,6},{8,9},{9,8},{10,11... | collective-permute-start | bytes 884744 | tf_op jit(solution)/shard_map/ppermute | solution.py:60
  105.3 18.7 %collective-permute-start.15 = (bf16[256,768]{1,0:T(8,128)(2,1)S(1)}, bf16[256,768]{1,0:T(8,128)(2,1)S(1)}, u32[]{:S(2)}, u32[]{:S(2)}) collective-permute-start(bf16[256,768]{1,0:T(8,128)(2,1)S(1)} %multiply_convert_fusion.1), channel_id=1, source_target_pairs={{0,1},{1,0},{2,3},{3,2},{4,5},{5,4},{6,7},{7,6},{8,9},{9,8},{10,11... | collective-permute-start | bytes 1179656 | tf_op jit(solution)/shard_map/ppermute | solution.py:60
  133.8 22.5 %collective-permute-start.21 = (bf16[256,768]{1,0:T(8,128)(2,1)}, bf16[256,768]{1,0:T(8,128)(2,1)}, u32[]{:S(2)}, u32[]{:S(2)}) collective-permute-start(bf16[256,768]{1,0:T(8,128)(2,1)} %slice.332), channel_id=1, source_target_pairs={{0,2},{1,3},{2,0},{3,1},{4,6},{5,7},{6,4},{7,5},{8,10},{9,11},{10,... | collective-permute-start | bytes 1179656 | tf_op jit(solution)/shard_map/ppermute | solution.py:60
  138.0 17.0 %collective-permute-start.27 = (bf16[128,768]{1,0:T(8,128)(2,1)}, bf16[128,768]{1,0:T(8,128)(2,1)}, u32[]{:S(2)}, u32[]{:S(2)}) collective-permute-start(bf16[128,768]{1,0:T(8,128)(2,1)} %get-tuple-element.126), channel_id=1, source_target_pairs={{0,4},{1,20},{2,12},{3,28},{4,0},{5,16},{6,8},{7,24},{8,6},{9,22},... | collective-permute-start | bytes 589832 | tf_op jit(solution)/shard_map/ppermute | solution.py:356
  138.7 17.6 %collective-permute-start.26 = (bf16[128,768]{1,0:T(8,128)(2,1)}, bf16[128,768]{1,0:T(8,128)(2,1)}, u32[]{:S(2)}, u32[]{:S(2)}) collective-permute-start(bf16[128,768]{1,0:T(8,128)(2,1)} %get-tuple-element.125), channel_id=1, source_target_pairs={{0,0},{1,16},{2,8},{3,24},{4,4},{5,20},{6,12},{7,28},{8,2},{9,18},... | collective-permute-start | bytes 589832 | tf_op jit(solution)/shard_map/ppermute | solution.py:355
  167.8 94.9 %collective-permute-start.23 = (bf16[128,768]{1,0:T(8,128)(2,1)S(1)}, bf16[128,768]{1,0:T(8,128)(2,1)S(1)}, u32[]{:S(2)}, u32[]{:S(2)}) collective-permute-start(bf16[128,768]{1,0:T(8,128)(2,1)S(1)} %get-tuple-element.128), channel_id=1, source_target_pairs={{4,0},{20,1},{12,2},{28,3},{0,4},{16,5},{8,6},{24,7},{6,8},{22,9},... | collective-permute-start | bytes 589832 | tf_op jit(solution)/shard_map/ppermute | solution.py:361
  177.9 16.3 %collective-permute-start.59 = (bf16[4,4,24,768]{3,2,1,0:T(8,128)(2,1)S(1)}, bf16[4,4,24,768]{3,2,1,0:T(8,128)(2,1)S(1)}, u32[]{:S(2)}, u32[]{:S(2)}) collective-permute-start(bf16[4,4,24,768]{3,2,1,0:T(8,128)(2,1)S(1)} %fusion.23), channel_id=1, source_target_pairs={{0,4},{4,0},{8,12},{12,8},{16,20},{20,16},{24,28},{28,24},{1,5},{5... | collective-permute-start | bytes 1769480 | tf_op jit(solution)/shard_map/ppermute | solution.py:65
  181.8 24.9 %collective-permute-start.70 = (bf16[4,96,768]{2,1,0:T(8,128)(2,1)S(1)}, bf16[4,96,768]{2,1,0:T(8,128)(2,1)S(1)}, u32[]{:S(2)}, u32[]{:S(2)}) collective-permute-start(bf16[4,96,768]{2,1,0:T(8,128)(2,1)S(1)} %fusion.24), channel_id=1, source_target_pairs={{0,4},{4,0},{8,12},{12,8},{16,20},{20,16},{24,28},{28,24},{1,5},{5... | collective-permute-start | bytes 1769480 | tf_op jit(solution)/shard_map/ppermute | solution.py:65
  184.2 44.8 %collective-permute-start.31 = (bf16[512,768]{1,0:T(8,128)(2,1)S(1)}, bf16[512,768]{1,0:T(8,128)(2,1)S(1)}, u32[]{:S(2)}, u32[]{:S(2)}) collective-permute-start(bf16[512,768]{1,0:T(8,128)(2,1)S(1)} %slice.328), channel_id=1, source_target_pairs={{0,1},{1,0},{2,3},{3,2},{4,5},{5,4},{6,7},{7,6},{8,9},{9,8},{10,11... | collective-permute-start | bytes 2359304 | tf_op jit(solution)/shard_map/ppermute | solution.py:60
  208.7 14.7 %collective-permute-start.72 = (bf16[96,768]{1,0:T(8,128)(2,1)S(1)}, bf16[96,768]{1,0:T(8,128)(2,1)S(1)}, u32[]{:S(2)}, u32[]{:S(2)}) collective-permute-start(bf16[96,768]{1,0:T(8,128)(2,1)S(1)} %get-tuple-element.76), channel_id=1, source_target_pairs={{0,16},{4,20},{8,24},{12,28},{16,0},{20,4},{24,8},{28,12},{1,17},{... | collective-permute-start | bytes 442376 | tf_op jit(solution)/shard_map/ppermute | solution.py:65
  227.4 18.2 %collective-permute-start.75 = (bf16[96,768]{1,0:T(8,128)(2,1)S(1)}, bf16[96,768]{1,0:T(8,128)(2,1)S(1)}, u32[]{:S(2)}, u32[]{:S(2)}) collective-permute-start(bf16[96,768]{1,0:T(8,128)(2,1)S(1)} %fusion.49), channel_id=1, source_target_pairs={{0,16},{4,20},{8,24},{12,28},{16,0},{20,4},{24,8},{28,12},{1,17},{... | collective-permute-start | bytes 442376 | tf_op jit(solution)/shard_map/ppermute | solution.py:65
  227.4 18.2 %collective-permute-start.74 = (bf16[96,768]{1,0:T(8,128)(2,1)S(1)}, bf16[96,768]{1,0:T(8,128)(2,1)S(1)}, u32[]{:S(2)}, u32[]{:S(2)}) collective-permute-start(bf16[96,768]{1,0:T(8,128)(2,1)S(1)} %fusion.49), channel_id=1, source_target_pairs={{0,8},{4,12},{8,0},{12,4},{16,24},{20,28},{24,16},{28,20},{1,9},{5... | collective-permute-start | bytes 442376 | tf_op jit(solution)/shard_map/ppermute | solution.py:65
  229.1 19.0 %collective-permute-start.68 = (bf16[24,4,768]{2,0,1:T(8,128)(2,1)S(1)}, bf16[24,4,768]{2,0,1:T(8,128)(2,1)S(1)}, u32[]{:S(2)}, u32[]{:S(2)}) collective-permute-start(bf16[24,4,768]{2,0,1:T(8,128)(2,1)S(1)} %get-tuple-element.141), channel_id=1, source_target_pairs={{0,24},{4,28},{8,16},{12,20},{16,8},{20,12},{24,0},{28,4},{1,25},{... | collective-permute-start | bytes 442376 | tf_op jit(solution)/shard_map/ppermute | solution.py:65
  233.0 20.2 %collective-permute-start.67 = (bf16[24,4,768]{2,0,1:T(8,128)(2,1)S(1)}, bf16[24,4,768]{2,0,1:T(8,128)(2,1)S(1)}, u32[]{:S(2)}, u32[]{:S(2)}) collective-permute-start(bf16[24,4,768]{2,0,1:T(8,128)(2,1)S(1)} %get-tuple-element.141), channel_id=1, source_target_pairs={{0,16},{4,20},{8,24},{12,28},{16,0},{20,4},{24,8},{28,12},{1,17},{... | collective-permute-start | bytes 442376 | tf_op jit(solution)/shard_map/ppermute | solution.py:65
  248.1 14.5 %collective-permute-start.22 = (bf16[128,768]{1,0:T(8,128)(2,1)S(1)}, bf16[128,768]{1,0:T(8,128)(2,1)S(1)}, u32[]{:S(2)}, u32[]{:S(2)}) collective-permute-start(bf16[128,768]{1,0:T(8,128)(2,1)S(1)} %get-tuple-element.127), channel_id=1, source_target_pairs={{0,0},{16,1},{8,2},{24,3},{4,4},{20,5},{12,6},{28,7},{2,8},{18,9},... | collective-permute-start | bytes 589832 | tf_op jit(solution)/shard_map/ppermute | solution.py:360
  253.1 16.3 %collective-permute-start.77 = (bf16[4,96,768]{2,1,0:T(8,128)(2,1)S(1)}, bf16[4,96,768]{2,1,0:T(8,128)(2,1)S(1)}, u32[]{:S(2)}, u32[]{:S(2)}) collective-permute-start(bf16[4,96,768]{2,1,0:T(8,128)(2,1)S(1)} %get-tuple-element.104), channel_id=1, source_target_pairs={{0,4},{4,0},{8,12},{12,8},{16,20},{20,16},{24,28},{28,24},{1,5},{5... | collective-permute-start | bytes 1769480 | tf_op jit(solution)/shard_map/ppermute | solution.py:65
  253.6 26.3 %collective-permute-start.69 = (bf16[4,24,4,768]{3,1,2,0:T(8,128)(2,1)S(1)}, bf16[4,24,4,768]{3,1,2,0:T(8,128)(2,1)S(1)}, u32[]{:S(2)}, u32[]{:S(2)}) collective-permute-start(bf16[4,24,4,768]{3,1,2,0:T(8,128)(2,1)S(1)} %get-tuple-element.110), channel_id=1, source_target_pairs={{0,4},{4,0},{8,12},{12,8},{16,20},{20,16},{24,28},{28,24},{1,5},{5... | collective-permute-start | bytes 1769480 | tf_op jit(solution)/shard_map/ppermute | solution.py:65
  263.5 19.7 %collective-permute-start.34 = (bf16[256,768]{1,0:T(8,128)(2,1)S(1)}, bf16[256,768]{1,0:T(8,128)(2,1)S(1)}, u32[]{:S(2)}, u32[]{:S(2)}) collective-permute-start(bf16[256,768]{1,0:T(8,128)(2,1)S(1)} %get-tuple-element.62), channel_id=1, source_target_pairs={{0,1},{1,0},{2,3},{3,2},{4,5},{5,4},{6,7},{7,6},{8,9},{9,8},{10,11... | collective-permute-start | bytes 1179656 | tf_op jit(solution)/shard_map/ppermute | solution.py:60
  283.7 20.7 %collective-permute-start.51 = (bf16[4,24,768]{2,1,0:T(8,128)(2,1)S(1)}, bf16[4,24,768]{2,1,0:T(8,128)(2,1)S(1)}, u32[]{:S(2)}, u32[]{:S(2)}) collective-permute-start(bf16[4,24,768]{2,1,0:T(8,128)(2,1)S(1)} %fusion.60), channel_id=1, source_target_pairs={{0,4},{4,0},{8,12},{12,8},{16,20},{20,16},{24,28},{28,24},{1,5},{5... | collective-permute-start | bytes 442376 | tf_op jit(solution)/shard_map/ppermute | solution.py:65
  318.8 35.7 %collective-permute-start.36 = (bf16[512,768]{1,0:T(8,128)(2,1)S(1)}, bf16[512,768]{1,0:T(8,128)(2,1)S(1)}, u32[]{:S(2)}, u32[]{:S(2)}) collective-permute-start(bf16[512,768]{1,0:T(8,128)(2,1)S(1)} %slice.327), channel_id=1, source_target_pairs={{0,1},{1,0},{2,3},{3,2},{4,5},{5,4},{6,7},{7,6},{8,9},{9,8},{10,11... | collective-permute-start | bytes 2359304 | tf_op jit(solution)/shard_map/ppermute | solution.py:60
  355.5 25.4 %collective-permute-start.37 = (bf16[256,768]{1,0:T(8,128)(2,1)}, bf16[256,768]{1,0:T(8,128)(2,1)S(1)}, u32[]{:S(2)}, u32[]{:S(2)}) collective-permute-start(bf16[256,768]{1,0:T(8,128)(2,1)} %slice.330), channel_id=1, source_target_pairs={{0,2},{1,3},{2,0},{3,1},{4,6},{5,7},{6,4},{7,5},{8,10},{9,11},{10,... | collective-permute-start | bytes 1179656 | tf_op jit(solution)/shard_map/ppermute | solution.py:60
  382.4 52.7 %collective-permute-start.39 = (bf16[128,768]{1,0:T(8,128)(2,1)S(1)}, bf16[128,768]{1,0:T(8,128)(2,1)S(1)}, u32[]{:S(2)}, u32[]{:S(2)}) collective-permute-start(bf16[128,768]{1,0:T(8,128)(2,1)S(1)} %get-tuple-element.123), channel_id=1, source_target_pairs={{4,0},{20,1},{12,2},{28,3},{0,4},{16,5},{8,6},{24,7},{6,8},{22,9},... | collective-permute-start | bytes 589832 | tf_op jit(solution)/shard_map/ppermute | solution.py:361
  382.5 52.6 %collective-permute-start.38 = (bf16[128,768]{1,0:T(8,128)(2,1)S(1)}, bf16[128,768]{1,0:T(8,128)(2,1)S(1)}, u32[]{:S(2)}, u32[]{:S(2)}) collective-permute-start(bf16[128,768]{1,0:T(8,128)(2,1)S(1)} %get-tuple-element.122), channel_id=1, source_target_pairs={{0,0},{16,1},{8,2},{24,3},{4,4},{20,5},{12,6},{28,7},{2,8},{18,9},... | collective-permute-start | bytes 589832 | tf_op jit(solution)/shard_map/ppermute | solution.py:360
  (89 other events, 852.3 us)
